TPU v7x, 32 devices: a whole 2x2x4 slice. The times are simulated.
32 devices in a mesh: fsdp: 4 (over y, x), ctx: 8 (over z, core).
Axes of the slice: x: 2, y: 2, z: 4, core: 2. Of those that a mesh axis runs over, the one named last changes fastest.
Arguments:
- inputs: bfloat16 [4096, 768], P(('fsdp', 'ctx')), may hold values from -6 to 6
- segments: int32 [4, 1024], P('fsdp'), may hold values from 0 to 7, as said below
- positions: int32 [4, 1024], P('fsdp', 'ctx'), may hold values from 0 to 383, as said below
- attention_norm_gain: bfloat16 [768], P(('fsdp', 'ctx')), may hold values from 0.5 to 1.5
- query_key_value_weight: bfloat16 [768, 2304], P(('fsdp', 'ctx')), may hold values from -2.7063294 to 2.7063294
- attention_output_weight: bfloat16 [768, 768], P(('fsdp', 'ctx')), may hold values from -4 to 4
- feedforward_norm_gain: bfloat16 [768], P(('fsdp', 'ctx')), may hold values from 0.5 to 1.5
- input_projection_weight: bfloat16 [768, 2304], P(('fsdp', 'ctx')), may hold values from -0.21875 to 0.21875
- down_projection_weight: bfloat16 [768, 1152], P(('fsdp', 'ctx')), may hold values from -0.25 to 0.25
- cotangent: bfloat16 [4096, 768], P(('fsdp', 'ctx')), may hold values from -6 to 6
Outputs:
- outputs: bfloat16 [4096, 768], P(('fsdp', 'ctx'))
- input_grad: bfloat16 [4096, 768], P(('fsdp', 'ctx'))
- attn_gain_grad: float32 [768], P(('fsdp', 'ctx'))
- qkv_weight_grad: float32 [768, 2304], P(('fsdp', 'ctx'))
- out_weight_grad: float32 [768, 768], P(('fsdp', 'ctx'))
- mlp_gain_grad: float32 [768], P(('fsdp', 'ctx'))
- in_weight_grad: float32 [768, 2304], P(('fsdp', 'ctx'))
- down_weight_grad: float32 [768, 1152], P(('fsdp', 'ctx'))
Inputs may be any that keep to these rules, and one draw needn't show every extreme that they name: `segments`: each row is cut into documents of consecutive tokens, each of 1 to 384 tokens, whose numbers rise along the row; the first document is number 0 and the last is number 1024 / 128 - 1; one document of each row has exactly 384 tokens. `positions`: the position of each token within its document, counting from 0.
All inputs are finite; a program needn't handle non-finite values.
Results may differ from a plain program's by a relative error of at most 0.04.
Values may be sent and summed in bfloat16 or wider, within the bound.
No kernel may reach another device: no remote copies, remote signals or barrier semaphores. Data moves between devices by JAX's collectives and lax.ppermute only.
A program may use at most 128 MiB of HBM per device.

v0:
```python
import math

import jax
import jax.numpy as jnp
from jax import lax
from jax.sharding import PartitionSpec as P

HEAD = 64
FF = 1152
LONGEST_DOCUMENT = 384


THETA = 160000.0
EPS = 1e-05
NEG = -1e30
SQRT_HALF = 0.7071067811865476
INV_SQRT_TAU = 0.3989422804014327


def shifted(value, axis, steps):
    count = lax.axis_size(axis)
    initial, last = (max(0, -steps), min(count, count - steps))
    return lax.ppermute(value, axis, [(source, source + steps) for source in range(initial, last)])


def layer_norm(values, gain):
    row_mean = jnp.mean(values, axis=-1, keepdims=True)
    centred = values - row_mean
    variance = jnp.mean(centred * centred, axis=-1, keepdims=True)
    inv_std = lax.rsqrt(variance + EPS)
    normed = centred * inv_std
    return (normed * gain, normed, inv_std)


def norm_back(grad_out, normed, inv_std, gain):
    grad_normed = grad_out * gain
    grad_gain = jnp.sum(grad_out * normed, axis=0)
    first_mean = jnp.mean(grad_normed, axis=-1, keepdims=True)
    second_mean = jnp.mean(grad_normed * normed, axis=-1, keepdims=True)
    return (inv_std * (grad_normed - first_mean - normed * second_mean), grad_gain)


def gelu_parts(values):
    normal_cdf = 0.5 * (1.0 + lax.erf(values * SQRT_HALF))
    slope = normal_cdf + values * jnp.exp(-0.5 * values * values) * INV_SQRT_TAU
    return (values * normal_cdf, slope)


def rope_tables(where):
    half_dim = HEAD // 2
    freq = THETA ** (-(jnp.arange(half_dim).astype(jnp.float32) * (2.0 / HEAD)))
    angles = where.astype(jnp.float32)[:, None] * freq[None, :]
    cosine = jnp.cos(angles)
    sine = jnp.sin(angles)
    return (
        jnp.concatenate([cosine, cosine], -1)[:, None, :],
        jnp.concatenate([sine, sine], -1)[:, None, :],
    )


def rotate(values, cosine, sine):
    half_dim = HEAD // 2
    turned = jnp.concatenate([-values[..., half_dim:], values[..., :half_dim]], -1)
    return values * cosine + turned * sine


def unrotate(grads, cosine, sine):
    half_dim = HEAD // 2
    scaled = grads * sine
    turned = jnp.concatenate([scaled[..., half_dim:], -scaled[..., :half_dim]], -1)
    return grads * cosine + turned


def masked_scores(query_rows, key_rows, query_segs, key_segs, scale_factor):
    scores = (
        jnp.einsum("qhd,khd->hqk", query_rows, key_rows, preferred_element_type=jnp.float32)
        * scale_factor
    )
    allowed = (query_segs[:, None] == key_segs[None, :])[None]
    return (jnp.where(allowed, scores, NEG), allowed)


def local(
    inputs,
    segments,
    positions,
    attention_norm_gain,
    query_key_value_weight,
    attention_output_weight,
    feedforward_norm_gain,
    input_projection_weight,
    down_projection_weight,
    cotangent,
):
    tok_rows, width = inputs.shape
    heads = width // HEAD
    scale_factor = HEAD ** (-0.5)
    qkv_full, out_full, attn_gain_full = (
        lax.all_gather(query_key_value_weight, ("fsdp", "ctx"), axis=0, tiled=True),
        lax.all_gather(attention_output_weight, ("fsdp", "ctx"), axis=0, tiled=True),
        lax.all_gather(attention_norm_gain, ("fsdp", "ctx"), axis=0, tiled=True),
    )
    in_full, down_full, mlp_gain_full = (
        lax.all_gather(input_projection_weight, ("fsdp", "ctx"), axis=0, tiled=True),
        lax.all_gather(down_projection_weight, ("fsdp", "ctx"), axis=0, tiled=True),
        lax.all_gather(feedforward_norm_gain, ("fsdp", "ctx"), axis=0, tiled=True),
    )
    attn_gain_f = attn_gain_full.astype(jnp.float32)
    mlp_gain_f = mlp_gain_full.astype(jnp.float32)
    row_segs = segments[0]
    reach = LONGEST_DOCUMENT // tok_rows
    own_index = lax.axis_index("ctx")
    own_segs = lax.dynamic_slice_in_dim(row_segs, own_index * tok_rows, tok_rows)
    window_len = (2 * reach + 1) * tok_rows
    padding = jnp.full((reach * tok_rows,), -1, jnp.int32)
    padded_segs = jnp.concatenate([padding, row_segs, padding])
    window_segs = lax.dynamic_slice_in_dim(padded_segs, own_index * tok_rows, window_len)
    x_float = inputs.astype(jnp.float32)
    attn_scaled, attn_normed, attn_inv = layer_norm(x_float, attn_gain_f)
    attn_input = attn_scaled.astype(jnp.bfloat16)
    qkv_rows = jnp.dot(attn_input, qkv_full, preferred_element_type=jnp.float32)
    cosine, sine = rope_tables(positions[0])
    query = rotate(qkv_rows[:, :width].reshape(tok_rows, heads, HEAD), cosine, sine).astype(
        jnp.bfloat16
    )
    key_own = rotate(
        qkv_rows[:, width : 2 * width].reshape(tok_rows, heads, HEAD), cosine, sine
    ).astype(jnp.bfloat16)
    key_flat = key_own.reshape(tok_rows, width)
    value_own = qkv_rows[:, 2 * width :].astype(jnp.bfloat16)
    key_pieces = []
    value_pieces = []
    for relative in range(-reach, reach + 1):
        if relative == 0:
            key_pieces.append(key_flat)
            value_pieces.append(value_own)
        else:
            got_key, got_value = shifted((key_flat, value_own), "ctx", -relative)
            key_pieces.append(got_key)
            value_pieces.append(got_value)
    key_window = jnp.concatenate(key_pieces, axis=0)
    value_window = jnp.concatenate(value_pieces, axis=0)
    block = math.gcd(window_len, 512)
    blocks = window_len // block
    key_blocks = key_window.reshape(blocks, block, heads, HEAD)
    value_blocks = value_window.reshape(blocks, block, heads, HEAD)
    seg_blocks = window_segs.reshape(blocks, block)

    def forward_step(carry, pieces):
        run_max, run_sum, accum = carry
        key_blk, value_blk, seg_blk = pieces
        scores, allowed = masked_scores(query, key_blk, own_segs, seg_blk, scale_factor)
        new_max = jnp.maximum(run_max, jnp.max(scores, axis=-1))
        rescale = jnp.exp(run_max - new_max)
        weights = jnp.where(allowed, jnp.exp(scores - new_max[..., None]), 0.0)
        run_sum = run_sum * rescale + jnp.sum(weights, axis=-1)
        accum = accum * jnp.transpose(rescale)[:, :, None] + jnp.einsum(
            "hqk,khd->qhd",
            weights.astype(jnp.bfloat16),
            value_blk,
            preferred_element_type=jnp.float32,
        )
        return ((new_max, run_sum, accum), None)

    start_max = jnp.full((heads, tok_rows), NEG, jnp.float32)
    start_sum = jnp.zeros((heads, tok_rows), jnp.float32)
    start_acc = jnp.zeros((tok_rows, heads, HEAD), jnp.float32)
    (run_max, run_sum, accum), unused = lax.scan(
        forward_step, (start_max, start_sum, start_acc), (key_blocks, value_blocks, seg_blocks)
    )
    lse = run_max + jnp.log(run_sum)
    attn_vec = (
        (accum / jnp.transpose(run_sum)[:, :, None]).reshape(tok_rows, width).astype(jnp.bfloat16)
    )
    attn_proj = jnp.dot(attn_vec, out_full, preferred_element_type=jnp.float32)
    resid = x_float + attn_proj
    mlp_scaled, mlp_normed, mlp_inv = layer_norm(resid, mlp_gain_f)
    mlp_input = mlp_scaled.astype(jnp.bfloat16)
    up_rows = jnp.dot(mlp_input, in_full, preferred_element_type=jnp.float32)
    gate_in = up_rows[:, :FF]
    gate_mul = up_rows[:, FF:]
    gelu_value, gelu_slope = gelu_parts(gate_in)
    hidden = (gelu_value * gate_mul).astype(jnp.bfloat16)
    outputs = (
        resid + jnp.einsum("tf,df->td", hidden, down_full, preferred_element_type=jnp.float32)
    ).astype(jnp.bfloat16)
    down_grad = jnp.einsum("td,tf->df", cotangent, hidden, preferred_element_type=jnp.float32)
    grad_hidden = jnp.einsum("td,df->tf", cotangent, down_full, preferred_element_type=jnp.float32)
    grad_up = jnp.concatenate(
        [grad_hidden * gate_mul * gelu_slope, grad_hidden * gelu_value], axis=1
    ).astype(jnp.bfloat16)
    in_grad = jnp.einsum("td,tf->df", mlp_input, grad_up, preferred_element_type=jnp.float32)
    grad_mlp_input = jnp.einsum("tf,df->td", grad_up, in_full, preferred_element_type=jnp.float32)
    grad_resid_n, mlp_gain_grad = norm_back(grad_mlp_input, mlp_normed, mlp_inv, mlp_gain_f)
    in_part, down_part, mlp_gain_part = (
        lax.psum_scatter(in_grad, ("fsdp", "ctx"), scatter_dimension=0, tiled=True),
        lax.psum_scatter(down_grad, ("fsdp", "ctx"), scatter_dimension=0, tiled=True),
        lax.psum_scatter(mlp_gain_grad, ("fsdp", "ctx"), scatter_dimension=0, tiled=True),
    )
    grad_resid = cotangent.astype(jnp.float32) + grad_resid_n
    grad_resid_low = grad_resid.astype(jnp.bfloat16)
    out_grad = jnp.einsum("td,te->de", attn_vec, grad_resid_low, preferred_element_type=jnp.float32)
    grad_vec = jnp.einsum(
        "te,de->td", grad_resid_low, out_full, preferred_element_type=jnp.float32
    ).astype(jnp.bfloat16)
    grad_heads = grad_vec.reshape(tok_rows, heads, HEAD)
    delta = jnp.transpose(
        jnp.sum(
            (grad_vec.astype(jnp.float32) * attn_vec.astype(jnp.float32)).reshape(
                tok_rows, heads, HEAD
            ),
            axis=-1,
        )
    )

    def query_step(grad_query, pieces):
        key_blk, value_blk, seg_blk = pieces
        scores, allowed = masked_scores(query, key_blk, own_segs, seg_blk, scale_factor)
        probs = jnp.where(allowed, jnp.exp(scores - lse[..., None]), 0.0)
        grad_probs = jnp.einsum(
            "qhd,khd->hqk", grad_heads, value_blk, preferred_element_type=jnp.float32
        )
        grad_scores = (probs * (grad_probs - delta[..., None]) * scale_factor).astype(jnp.bfloat16)
        grad_query = grad_query + jnp.einsum(
            "hqk,khd->qhd", grad_scores, key_blk, preferred_element_type=jnp.float32
        )
        grad_value = jnp.einsum(
            "hqk,qhd->khd",
            probs.astype(jnp.bfloat16),
            grad_heads,
            preferred_element_type=jnp.float32,
        )
        grad_key = jnp.einsum(
            "hqk,qhd->khd", grad_scores, query, preferred_element_type=jnp.float32
        )
        return (grad_query, (grad_key, grad_value))

    query_grad, (key_parts, value_parts) = lax.scan(
        query_step, start_acc, (key_blocks, value_blocks, seg_blocks)
    )
    key_terms = key_parts.reshape(window_len, width)
    value_terms = value_parts.reshape(window_len, width)
    key_grad = key_terms[reach * tok_rows : (reach + 1) * tok_rows]
    value_grad = value_terms[reach * tok_rows : (reach + 1) * tok_rows]
    for relative in range(-reach, reach + 1):
        if relative != 0:
            lower = (relative + reach) * tok_rows
            got_key, got_value = (
                shifted(
                    key_terms[lower : lower + tok_rows].astype(jnp.bfloat16), "ctx", relative
                ).astype(jnp.float32),
                shifted(
                    value_terms[lower : lower + tok_rows].astype(jnp.bfloat16), "ctx", relative
                ).astype(jnp.float32),
            )
            key_grad = key_grad + got_key
            value_grad = value_grad + got_value
    query_back = unrotate(query_grad, cosine, sine).reshape(tok_rows, width)
    key_back = unrotate(key_grad.reshape(tok_rows, heads, HEAD), cosine, sine).reshape(
        tok_rows, width
    )
    grad_qkv = jnp.concatenate([query_back, key_back, value_grad], axis=1).astype(jnp.bfloat16)
    qkv_grad = jnp.einsum("td,te->de", attn_input, grad_qkv, preferred_element_type=jnp.float32)
    grad_attn_input = jnp.einsum(
        "te,de->td", grad_qkv, qkv_full, preferred_element_type=jnp.float32
    )
    grad_x_n, attn_gain_grad = norm_back(grad_attn_input, attn_normed, attn_inv, attn_gain_f)
    input_grad = (grad_resid + grad_x_n).astype(jnp.bfloat16)
    qkv_part, out_part, attn_gain_part = (
        lax.psum_scatter(qkv_grad, ("fsdp", "ctx"), scatter_dimension=0, tiled=True),
        lax.psum_scatter(out_grad, ("fsdp", "ctx"), scatter_dimension=0, tiled=True),
        lax.psum_scatter(attn_gain_grad, ("fsdp", "ctx"), scatter_dimension=0, tiled=True),
    )
    return (
        outputs,
        input_grad,
        attn_gain_part,
        qkv_part,
        out_part,
        mlp_gain_part,
        in_part,
        down_part,
    )


def solution(mesh):
    in_specs = (
        P(("fsdp", "ctx"), None),
        P("fsdp", None),
        P("fsdp", "ctx"),
        P(("fsdp", "ctx")),
        P(("fsdp", "ctx"), None),
        P(("fsdp", "ctx"), None),
        P(("fsdp", "ctx")),
        P(("fsdp", "ctx"), None),
        P(("fsdp", "ctx"), None),
        P(("fsdp", "ctx"), None),
    )
    out_specs = (
        P(("fsdp", "ctx"), None),
        P(("fsdp", "ctx"), None),
        P(("fsdp", "ctx")),
        P(("fsdp", "ctx"), None),
        P(("fsdp", "ctx"), None),
        P(("fsdp", "ctx")),
        P(("fsdp", "ctx"), None),
        P(("fsdp", "ctx"), None),
    )
    return jax.shard_map(local, mesh=mesh, in_specs=in_specs, out_specs=out_specs, check_vma=False)
```

profile of v0, /device:TPU:0, one launch (start us, length us, event | category | flops | bytes accessed | tf_op | source)
XLA Modules:
  0.0 756.3 jit_solution(16676608840963658987)
XLA Ops:
  14.6 42.3 %all-reduce.6 = (bf16[768]{0:T(1024)(128)(2,1)S(1)}, bf16[768]{0:T(1024)(128)(2,1)S(1)}) all-reduce(bf16[768]{0:T(1024)(128)(2,1)S(1)} %dynamic-update-slice, bf16[768]{0:T(1024)(128)(2,1)S(1)} %dynamic-update-slice.1), channel_id=1, replica_groups=mesh['fsdp'=4,'ctx'=8] {'fsdp','ctx'}, use_global_device_ids=true, to_apply=%add | all-reduce | flops 1536 | bytes 6144
  59.2 14.8 %all-gather.5.cloned.1.call-done = bf16[768,2304]{1,0:T(8,128)(2,1)} async-done(((bf16[24,2304]{1,0:T(8,128)(2,1)}), bf16[768,2304]{1,0:T(8,128)(2,1)}) %all-gather.5.cloned.1.call-update) | async-done | bytes 3538960 | tf_op jit(solution)/shard_map/all_gather | solution.py:99
  74.0 2.7 fusion.93
  80.0 3.7 collective-permute-start.8
  83.7 5.3 collective-permute-start.6
  93.0 4.8 collective-permute-done
  97.8 8.1 %collective-permute-start.1 = (bf16[128,768]{1,0:T(8,128)(2,1)}, bf16[128,768]{1,0:T(8,128)(2,1)S(1)}, u32[]{:S(2)}, u32[]{:S(2)}) collective-permute-start(bf16[128,768]{1,0:T(8,128)(2,1)} %get-tuple-element.354), channel_id=1, source_target_pairs={{0,2},{1,3},{2,4},{3,5},{4,6},{5,7},{8,10},{9,11},{10,12},{11,13},... | collective-permute-start | bytes 589832 | tf_op jit(solution)/shard_map/ppermute | solution.py:23
  123.3 5.6 collective-permute-done.3
  130.3 11.6 %collective-permute-done.5 = bf16[128,768]{1,0:T(8,128)(2,1)S(1)} collective-permute-done((bf16[128,768]{1,0:T(8,128)(2,1)}, bf16[128,768]{1,0:T(8,128)(2,1)S(1)}, u32[]{:S(2)}, u32[]{:S(2)}) %collective-permute-start.5) | collective-permute-done | bytes 196640 | tf_op jit(solution)/shard_map/ppermute | solution.py:23
  142.8 2.5 reshape.203
  153.7 2.5 reshape.205
  158.0 15.8 %while.30 = (s32[]{:T(128)}, f32[12,128]{1,0:T(8,128)S(1)}, f32[12,128]{1,0:T(8,128)S(1)}, f32[128,12,64]{0,2,1:T(8,128)S(1)}, s32[128]{0:T(128)}, /*index=5*/s3...) while((s32[]{:T(128)}, f32[12,128]{1,0:T(8,128)S(1)}, ...), condition=%wide.region_5.6_spmd.clone, body=%wide.region_2.5_spmd.clone.sunk | while | flops 52421632 | bytes 3905677 | solution.py:168
  177.7 15.0 %all-gather.9.cloned.1.call-done = bf16[768,2304]{1,0:T(8,128)(2,1)} async-done(((bf16[24,2304]{1,0:T(8,128)(2,1)}), bf16[768,2304]{1,0:T(8,128)(2,1)}) %all-gather.9.cloned.1.call-update) | async-done | bytes 3538960 | tf_op jit(solution)/shard_map/all_gather | solution.py:104
  192.8 2.7 fusion.95
  195.5 2.5 convolution_bitcast_fusion.4
  198.1 51.6 %all-gather.11.cloned.1.call-done = bf16[768,1152]{1,0:T(8,128)(2,1)} async-done(((bf16[24,1152]{1,0:T(8,128)(2,1)}), bf16[768,1152]{1,0:T(8,128)(2,1)}) %all-gather.11.cloned.1.call-update) | async-done | bytes 1769488 | tf_op jit(solution)/shard_map/all_gather | solution.py:105
  257.4 2.7 convert_multiply_fusion
  262.9 5.2 fusion.78
  268.8 34.9 %while.31 = (s32[]{:T(128)}, f32[128,12,64]{0,2,1:T(8,128)S(1)}, f32[7,128,12,64]{1,3,2,0:T(8,128)}, f32[7,128,12,64]{1,3,2,0:T(8,128)}, bf16[7,128,12,64]{1,3,2...) while((s32[]{:T(128)}, f32[128,12,64]{0,2,1:T(8,128)S(1)}, ...), condition=%wide.region_12.13_spmd.clone, body=%wide.region_11.12_spmd.clone.sunk | while | flops 127811584 | bytes 6537391 | solution.py:238
  311.0 2.8 collective-permute-start.16
  313.8 4.0 collective-permute-start.15
  320.6 6.2 collective-permute-start.23
  328.2 3.6 collective-permute-start.22
  331.8 4.1 collective-permute-start.21
  340.2 9.1 %collective-permute-done.19 = bf16[128,768]{0,1:T(8,128)(2,1)S(1)} collective-permute-done((bf16[128,768]{0,1:T(8,128)(2,1)S(1)}, bf16[128,768]{0,1:T(8,128)(2,1)S(1)}, u32[]{:S(2)}, u32[]{:S(2)}) %collective-permute-start.19) | collective-permute-done | bytes 196640 | tf_op jit(solution)/shard_map/ppermute | solution.py:23
  349.6 4.1 fusion.80
  355.0 2.8 fusion.42
  357.8 3.4 fusion.61
  361.2 40.0 %all-reduce.5 = (f32[768]{0:T(1024)S(1)}, f32[768]{0:T(1024)S(1)}) all-reduce(f32[768]{0:T(1024)S(1)} %get-tuple-element.285, f32[768]{0:T(1024)S(1)} %copy-done.29), channel_id=2, replica_groups=mesh['fsdp'=4,'ctx'=8] {'fsdp','ctx'}, use_global_device_ids=true, to_apply=%region_16.17.clone | all-reduce | flops 1536 | bytes 12288
  405.6 94.3 %reduce-scatter.7.cloned.1.call-done = f32[24,768]{1,0:T(8,128)} async-done(((f32[768,768]{1,0:T(8,128)}), f32[24,768]{1,0:T(8,128)}) %reduce-scatter.7.cloned.1.call-update) | async-done | bytes 73744 | tf_op jit(solution)/shard_map/reduce_scatter | solution.py:271
  499.9 124.8 %reduce-scatter.9.cloned.1.call-done = f32[24,2304]{1,0:T(8,128)} async-done(((f32[768,2304]{1,0:T(8,128)}), f32[24,2304]{1,0:T(8,128)}) %reduce-scatter.9.cloned.1.call-update) | async-done | bytes 221200 | tf_op jit(solution)/shard_map/reduce_scatter | solution.py:196
  624.7 124.8 %reduce-scatter.5.cloned.1.call-done = f32[24,2304]{1,0:T(8,128)} async-done(((f32[768,2304]{1,0:T(8,128)}), f32[24,2304]{1,0:T(8,128)}) %reduce-scatter.5.cloned.1.call-update) | async-done | bytes 221200 | tf_op jit(solution)/shard_map/reduce_scatter | solution.py:270
  (309 shorter events, 132.8 us)
Async XLA Ops:
  7.2 66.8 %all-gather.5.cloned.1.call-start = ((), (), s32[]{:S(2)}) async-start(), calls=%async_computation.3 | async-start | bytes 3649536 | tf_op jit(solution)/shard_map/all_gather | solution.py:99
  7.9 166.7 %all-gather.7.cloned.1.call-start = ((), (), s32[]{:S(2)}) async-start(), calls=%async_computation.4 | async-start | bytes 1216512 | tf_op jit(solution)/shard_map/all_gather | solution.py:100
  8.7 184.1 %all-gather.9.cloned.1.call-start = ((), (), s32[]{:S(2)}) async-start(), calls=%async_computation.5 | async-start | bytes 3649536 | tf_op jit(solution)/shard_map/all_gather | solution.py:104
  9.4 240.2 %all-gather.11.cloned.1.call-start = ((), (), s32[]{:S(2)}) async-start(), calls=%async_computation.6 | async-start | bytes 1824768 | tf_op jit(solution)/shard_map/all_gather | solution.py:105
  10.0 393.3 %all-reduce.9.cloned.1.call-start = ((), (), s32[]{:S(2)}) async-start(), calls=%async_computation.10 | async-start | bytes 7077888
  77.4 71.3 %collective-permute-start.10 = (bf16[128,768]{1,0:T(8,128)(2,1)}, bf16[128,768]{1,0:T(8,128)(2,1)}, u32[]{:S(2)}, u32[]{:S(2)}) collective-permute-start(bf16[128,768]{1,0:T(8,128)(2,1)} %slice.191), channel_id=1, source_target_pairs={{2,0},{3,1},{4,2},{5,3},{6,4},{7,5},{10,8},{11,9},{12,10},{13,11},... | collective-permute-start | bytes 589832 | tf_op jit(solution)/shard_map/ppermute | solution.py:23
  78.7 68.4 %collective-permute-start.9 = (bf16[128,768]{1,0:T(8,128)(2,1)}, bf16[128,768]{1,0:T(8,128)(2,1)}, u32[]{:S(2)}, u32[]{:S(2)}) collective-permute-start(bf16[128,768]{1,0:T(8,128)(2,1)} %slice.191), channel_id=1, source_target_pairs={{1,0},{2,1},{3,2},{4,3},{5,4},{6,5},{7,6},{9,8},{10,9},{11,10},{12... | collective-permute-start | bytes 589832 | tf_op jit(solution)/shard_map/ppermute | solution.py:23
  80.0 37.4 %collective-permute-start.8 = (bf16[128,768]{1,0:T(8,128)(2,1)}, bf16[128,768]{1,0:T(8,128)(2,1)}, u32[]{:S(2)}, u32[]{:S(2)}) collective-permute-start(bf16[128,768]{1,0:T(8,128)(2,1)} %slice.191), channel_id=1, source_target_pairs={{0,1},{1,2},{2,3},{3,4},{4,5},{5,6},{6,7},{8,9},{9,10},{10,11},{11... | collective-permute-start | bytes 589832 | tf_op jit(solution)/shard_map/ppermute | solution.py:23
  83.7 22.2 %collective-permute-start.6 = (bf16[128,768]{1,0:T(8,128)(2,1)}, bf16[128,768]{1,0:T(8,128)(2,1)}, u32[]{:S(2)}, u32[]{:S(2)}) collective-permute-start(bf16[128,768]{1,0:T(8,128)(2,1)} %slice.191), channel_id=1, source_target_pairs={{0,3},{1,4},{2,5},{3,6},{4,7},{8,11},{9,12},{10,13},{11,14},{12,15... | collective-permute-start | bytes 589832 | tf_op jit(solution)/shard_map/ppermute | solution.py:23
  90.4 7.4 collective-permute-start
  97.8 14.0 %collective-permute-start.1 = (bf16[128,768]{1,0:T(8,128)(2,1)}, bf16[128,768]{1,0:T(8,128)(2,1)S(1)}, u32[]{:S(2)}, u32[]{:S(2)}) collective-permute-start(bf16[128,768]{1,0:T(8,128)(2,1)} %get-tuple-element.354), channel_id=1, source_target_pairs={{0,2},{1,3},{2,4},{3,5},{4,6},{5,7},{8,10},{9,11},{10,12},{11,13},... | collective-permute-start | bytes 589832 | tf_op jit(solution)/shard_map/ppermute | solution.py:23
  105.9 9.5 %collective-permute-start.7 = (bf16[128,768]{1,0:T(8,128)(2,1)}, bf16[128,768]{1,0:T(8,128)(2,1)S(1)}, u32[]{:S(2)}, u32[]{:S(2)}) collective-permute-start(bf16[128,768]{1,0:T(8,128)(2,1)} %slice.191), channel_id=1, source_target_pairs={{0,2},{1,3},{2,4},{3,5},{4,6},{5,7},{8,10},{9,11},{10,12},{11,13},... | collective-permute-start | bytes 589832 | tf_op jit(solution)/shard_map/ppermute | solution.py:23
  111.8 38.5 %collective-permute-start.11 = (bf16[128,768]{1,0:T(8,128)(2,1)}, bf16[128,768]{1,0:T(8,128)(2,1)}, u32[]{:S(2)}, u32[]{:S(2)}) collective-permute-start(bf16[128,768]{1,0:T(8,128)(2,1)} %slice.191), channel_id=1, source_target_pairs={{3,0},{4,1},{5,2},{6,3},{7,4},{11,8},{12,9},{13,10},{14,11},{15,12... | collective-permute-start | bytes 589832 | tf_op jit(solution)/shard_map/ppermute | solution.py:23
  115.4 14.9 %collective-permute-start.4 = (bf16[128,768]{1,0:T(8,128)(2,1)}, bf16[128,768]{1,0:T(8,128)(2,1)S(1)}, u32[]{:S(2)}, u32[]{:S(2)}) collective-permute-start(bf16[128,768]{1,0:T(8,128)(2,1)} %get-tuple-element.354), channel_id=1, source_target_pairs={{2,0},{3,1},{4,2},{5,3},{6,4},{7,5},{10,8},{11,9},{12,10},{13,11},... | collective-permute-start | bytes 589832 | tf_op jit(solution)/shard_map/ppermute | solution.py:23
  117.4 3.7 collective-permute-start.2
  121.1 7.9 %collective-permute-start.3 = (bf16[128,768]{1,0:T(8,128)(2,1)}, bf16[128,768]{1,0:T(8,128)(2,1)S(1)}, u32[]{:S(2)}, u32[]{:S(2)}) collective-permute-start(bf16[128,768]{1,0:T(8,128)(2,1)} %get-tuple-element.354), channel_id=1, source_target_pairs={{1,0},{2,1},{3,2},{4,3},{5,4},{6,5},{7,6},{9,8},{10,9},{11,10},{12... | collective-permute-start | bytes 589832 | tf_op jit(solution)/shard_map/ppermute | solution.py:23
  129.0 12.9 %collective-permute-start.5 = (bf16[128,768]{1,0:T(8,128)(2,1)}, bf16[128,768]{1,0:T(8,128)(2,1)S(1)}, u32[]{:S(2)}, u32[]{:S(2)}) collective-permute-start(bf16[128,768]{1,0:T(8,128)(2,1)} %get-tuple-element.354), channel_id=1, source_target_pairs={{3,0},{4,1},{5,2},{6,3},{7,4},{11,8},{12,9},{13,10},{14,11},{15,12... | collective-permute-start | bytes 589832 | tf_op jit(solution)/shard_map/ppermute | solution.py:23
  198.0 301.9 %reduce-scatter.7.cloned.1.call-start = ((), (), s32[]{:S(2)}) async-start(), calls=%async_computation.8 | async-start | bytes 2433024 | tf_op jit(solution)/shard_map/reduce_scatter | solution.py:271
  256.9 367.8 %reduce-scatter.9.cloned.1.call-start = ((), (), s32[]{:S(2)}) async-start(), calls=%async_computation.9 | async-start | bytes 7299072 | tf_op jit(solution)/shard_map/reduce_scatter | solution.py:196
  268.1 481.4 %reduce-scatter.5.cloned.1.call-start = ((), (), s32[]{:S(2)}) async-start(), calls=%async_computation.7 | async-start | bytes 7299072 | tf_op jit(solution)/shard_map/reduce_scatter | solution.py:270
  306.0 13.1 %collective-permute-start.17 = (bf16[128,768]{0,1:T(8,128)(2,1)S(1)}, bf16[128,768]{0,1:T(8,128)(2,1)S(1)}, u32[]{:S(2)}, u32[]{:S(2)}) collective-permute-start(bf16[128,768]{0,1:T(8,128)(2,1)S(1)} %bitcast.220), channel_id=1, source_target_pairs={{0,3},{1,4},{2,5},{3,6},{4,7},{8,11},{9,12},{10,13},{11,14},{12,15... | collective-permute-start | bytes 589832 | tf_op jit(solution)/shard_map/ppermute | solution.py:23
  309.7 10.9 %collective-permute-start.12 = (bf16[128,768]{0,1:T(8,128)(2,1)S(1)}, bf16[128,768]{0,1:T(8,128)(2,1)S(1)}, u32[]{:S(2)}, u32[]{:S(2)}) collective-permute-start(bf16[128,768]{0,1:T(8,128)(2,1)S(1)} %bitcast.219), channel_id=1, source_target_pairs={{3,0},{4,1},{5,2},{6,3},{7,4},{11,8},{12,9},{13,10},{14,11},{15,12... | collective-permute-start | bytes 589832 | tf_op jit(solution)/shard_map/ppermute | solution.py:23
  311.0 15.8 %collective-permute-start.16 = (bf16[128,768]{0,1:T(8,128)(2,1)S(1)}, bf16[128,768]{0,1:T(8,128)(2,1)S(1)}, u32[]{:S(2)}, u32[]{:S(2)}) collective-permute-start(bf16[128,768]{0,1:T(8,128)(2,1)S(1)} %bitcast.218), channel_id=1, source_target_pairs={{0,2},{1,3},{2,4},{3,5},{4,6},{5,7},{8,10},{9,11},{10,12},{11,13},... | collective-permute-start | bytes 589832 | tf_op jit(solution)/shard_map/ppermute | solution.py:23
  313.8 14.4 %collective-permute-start.15 = (bf16[128,768]{0,1:T(8,128)(2,1)S(1)}, bf16[128,768]{0,1:T(8,128)(2,1)S(1)}, u32[]{:S(2)}, u32[]{:S(2)}) collective-permute-start(bf16[128,768]{0,1:T(8,128)(2,1)S(1)} %bitcast.217), channel_id=1, source_target_pairs={{0,1},{1,2},{2,3},{3,4},{4,5},{5,6},{6,7},{8,9},{9,10},{10,11},{11... | collective-permute-start | bytes 589832 | tf_op jit(solution)/shard_map/ppermute | solution.py:23
  317.8 14.0 %collective-permute-start.14 = (bf16[128,768]{0,1:T(8,128)(2,1)S(1)}, bf16[128,768]{0,1:T(8,128)(2,1)S(1)}, u32[]{:S(2)}, u32[]{:S(2)}) collective-permute-start(bf16[128,768]{0,1:T(8,128)(2,1)S(1)} %bitcast.216), channel_id=1, source_target_pairs={{1,0},{2,1},{3,2},{4,3},{5,4},{6,5},{7,6},{9,8},{10,9},{11,10},{12... | collective-permute-start | bytes 589832 | tf_op jit(solution)/shard_map/ppermute | solution.py:23
  319.1 16.8 %collective-permute-start.13 = (bf16[128,768]{0,1:T(8,128)(2,1)S(1)}, bf16[128,768]{0,1:T(8,128)(2,1)S(1)}, u32[]{:S(2)}, u32[]{:S(2)}) collective-permute-start(bf16[128,768]{0,1:T(8,128)(2,1)S(1)} %bitcast.215), channel_id=1, source_target_pairs={{2,0},{3,1},{4,2},{5,3},{6,4},{7,5},{10,8},{11,9},{12,10},{13,11},... | collective-permute-start | bytes 589832 | tf_op jit(solution)/shard_map/ppermute | solution.py:23
  320.6 17.7 %collective-permute-start.23 = (bf16[128,768]{0,1:T(8,128)(2,1)S(1)}, bf16[128,768]{0,1:T(8,128)(2,1)S(1)}, u32[]{:S(2)}, u32[]{:S(2)}) collective-permute-start(bf16[128,768]{0,1:T(8,128)(2,1)S(1)} %bitcast.214), channel_id=1, source_target_pairs={{0,3},{1,4},{2,5},{3,6},{4,7},{8,11},{9,12},{10,13},{11,14},{12,15... | collective-permute-start | bytes 589832 | tf_op jit(solution)/shard_map/ppermute | solution.py:23
  326.8 12.8 %collective-permute-start.18 = (bf16[128,768]{0,1:T(8,128)(2,1)S(1)}, bf16[128,768]{0,1:T(8,128)(2,1)S(1)}, u32[]{:S(2)}, u32[]{:S(2)}) collective-permute-start(bf16[128,768]{0,1:T(8,128)(2,1)S(1)} %bitcast.213), channel_id=1, source_target_pairs={{3,0},{4,1},{5,2},{6,3},{7,4},{11,8},{12,9},{13,10},{14,11},{15,12... | collective-permute-start | bytes 589832 | tf_op jit(solution)/shard_map/ppermute | solution.py:23
  328.2 11.5 %collective-permute-start.22 = (bf16[128,768]{0,1:T(8,128)(2,1)S(1)}, bf16[128,768]{0,1:T(8,128)(2,1)S(1)}, u32[]{:S(2)}, u32[]{:S(2)}) collective-permute-start(bf16[128,768]{0,1:T(8,128)(2,1)S(1)} %bitcast.212), channel_id=1, source_target_pairs={{0,2},{1,3},{2,4},{3,5},{4,6},{5,7},{8,10},{9,11},{10,12},{11,13},... | collective-permute-start | bytes 589832 | tf_op jit(solution)/shard_map/ppermute | solution.py:23
  331.8 7.9 %collective-permute-start.21 = (bf16[128,768]{0,1:T(8,128)(2,1)S(1)}, bf16[128,768]{0,1:T(8,128)(2,1)S(1)}, u32[]{:S(2)}, u32[]{:S(2)}) collective-permute-start(bf16[128,768]{0,1:T(8,128)(2,1)S(1)} %bitcast.211), channel_id=1, source_target_pairs={{0,1},{1,2},{2,3},{3,4},{4,5},{5,6},{6,7},{8,9},{9,10},{10,11},{11... | collective-permute-start | bytes 589832 | tf_op jit(solution)/shard_map/ppermute | solution.py:23
  335.9 4.3 collective-permute-start.20
  338.3 11.1 %collective-permute-start.19 = (bf16[128,768]{0,1:T(8,128)(2,1)S(1)}, bf16[128,768]{0,1:T(8,128)(2,1)S(1)}, u32[]{:S(2)}, u32[]{:S(2)}) collective-permute-start(bf16[128,768]{0,1:T(8,128)(2,1)S(1)} %bitcast.209), channel_id=1, source_target_pairs={{2,0},{3,1},{4,2},{5,3},{6,4},{7,5},{10,8},{11,9},{12,10},{13,11},... | collective-permute-start | bytes 589832 | tf_op jit(solution)/shard_map/ppermute | solution.py:23
  (30 other events, 453.4 us)
Sparse Core Ops, SparseCore 0:
  11.0 62.9 all-gather.4
  77.0 53.5 all-gather.6
  133.6 59.1 all-gather.8
  195.5 54.1 all-gather.10
  255.1 139.8 all-reduce.8
  400.7 99.1 reduce-scatter.6
  506.2 118.5 reduce-scatter.8
  631.0 118.4 reduce-scatter.4
where the time goes:
time: 759 us; the launch traced here: 756 us
  waiting for transfers between devices  464 us (61%)
  blocking collectives  82.3 us (11%)
  matrix products  67.7 us (9%)
  starting transfers between devices  62 us (8%)
  local copies, waits for them, and re-layouts  45.8 us (6%)
  other arithmetic  18.5 us (2%)
  between operations  15.1 us (2%)
    reduce_scatter x1, waiting for transfers between devices, local(): lax.psum_scatter(in_grad, ('fsdp', 'ctx'), scatter_dimension=0, tiled=True)  125 us
    reduce_scatter x1, waiting for transfers between devices, local(): lax.psum_scatter(qkv_grad, ('fsdp', 'ctx'), scatter_dimension=0, tiled=True)  125 us
    reduce_scatter x1, waiting for transfers between devices, local(): lax.psum_scatter(out_grad, ('fsdp', 'ctx'), scatter_dimension=0, tiled=True)  94.3 us
    unnamed x2, blocking collectives  82.3 us
    ppermute x24, starting transfers between devices, shifted(): lax.ppermute(value, axis, [(source, source + steps) for source in range(i...  61.5 us
    all_gather x1, waiting for transfers between devices, local(): lax.all_gather(down_projection_weight, ('fsdp', 'ctx'), axis=0, tiled=True)  51.6 us
    ppermute x24, waiting for transfers between devices, shifted(): lax.ppermute(value, axis, [(source, source + steps) for source in range(i...  36.3 us
    unnamed x82, local copies, waits for them, and re-layouts  21.5 us
  transfers between devices with their start and end apart: 32, of which 13 were waited for; matrix products, arithmetic and copies ran while one was open for 17% of the time, Pallas kernels for 0%

commit v1 on v0

v1 whole, which is shorter than its diff:
```python
import functools
import math

import jax
import jax.numpy as jnp
from jax import lax
from jax.experimental import pallas as pl
from jax.experimental.pallas import tpu as pltpu
from jax.sharding import PartitionSpec as P

HEAD = 64
FF = 1152
LONGEST_DOCUMENT = 384
LANES = 128
HEADS_STEP = 4
GROUP = HEADS_STEP * HEAD

THETA = 160000.0
EPS = 1e-05
NEG = -1e30
SQRT_HALF = 0.7071067811865476
INV_SQRT_TAU = 0.3989422804014327
AXES = ("fsdp", "ctx")
BF = jnp.bfloat16
F32 = jnp.float32


def exchange_groups(fsdp, ctx):
    bits = ctx.bit_length() - 1
    groups = []
    for low in range(1, bits, 2):
        high = min(low + 2, bits)
        groups.append([j << low for j in range(1 << (high - low))])
    groups.append([j * ctx for j in range(fsdp)])
    groups.append([0, 1])
    return groups


def slot_masks(groups):
    masks = [0]
    for group in groups:
        masks = [outer ^ inner for outer in group for inner in masks]
    return masks


def xor_permute(value, mask, count):
    return lax.ppermute(value, AXES, [(d, d ^ mask) for d in range(count)])


def gather_rows(shard, groups, count):
    held = shard
    for group in groups[:-1]:
        held = jnp.concatenate(
            [held] + [xor_permute(held, m, count) for m in group[1:]], axis=0
        )
    return held, xor_permute(held, groups[-1][1], count)


def scatter_rows(kept, sent, groups, count):
    held = kept + xor_permute(sent, groups[-1][1], count).astype(F32)
    for group in reversed(groups[:-1]):
        rows = held.shape[0] // len(group)
        total = held[:rows]
        for j, mask in enumerate(group):
            if j:
                part = held[j * rows : (j + 1) * rows].astype(BF)
                total = total + xor_permute(part, mask, count).astype(F32)
        held = total
    return held


def shifted(value, steps):
    ctx = lax.axis_size("ctx")
    first, last = max(0, -steps), min(ctx, ctx - steps)
    return lax.ppermute(value, "ctx", [(s, s + steps) for s in range(first, last)])


def dot(a, b):
    return jnp.dot(a, b, preferred_element_type=F32)


def dot_nt(a, b):
    return lax.dot_general(a, b, (((1,), (1,)), ((), ())), preferred_element_type=F32)


def dot_tn(a, b):
    return lax.dot_general(a, b, (((0,), (0,)), ((), ())), preferred_element_type=F32)


def layer_norm(values, gain):
    row_mean = jnp.mean(values, axis=-1, keepdims=True)
    centred = values - row_mean
    variance = jnp.mean(centred * centred, axis=-1, keepdims=True)
    inv_std = lax.rsqrt(variance + EPS)
    normed = centred * inv_std
    return (normed * gain, normed, inv_std)


def norm_back(grad_out, normed, inv_std, gain):
    grad_normed = grad_out * gain
    first_mean = jnp.mean(grad_normed, axis=-1, keepdims=True)
    second_mean = jnp.mean(grad_normed * normed, axis=-1, keepdims=True)
    return inv_std * (grad_normed - first_mean - normed * second_mean)


def gelu_parts(values):
    normal_cdf = 0.5 * (1.0 + lax.erf(values * SQRT_HALF))
    slope = normal_cdf + values * jnp.exp(-0.5 * values * values) * INV_SQRT_TAU
    return (values * normal_cdf, slope)


def rope_tables(where):
    lane = jnp.arange(LANES) % (HEAD // 2)
    freq = THETA ** (-(lane.astype(F32) * (2.0 / HEAD)))
    angles = where.astype(F32)[:, None] * freq[None, :]
    return jnp.cos(angles), jnp.sin(angles)


def half_sign(shape):
    lane = lax.broadcasted_iota(jnp.int32, shape, len(shape) - 1)
    return (lane % HEAD) < HEAD // 2


def swapped(values):
    half = HEAD // 2
    low = half_sign(values.shape)
    width = values.shape[-1]
    up = pltpu.roll(values, width - half, 1)
    down = pltpu.roll(values, half, 1)
    return low, jnp.where(low, up, down)


def rotate(values, cosine, sine):
    low, other = swapped(values)
    return values * cosine + jnp.where(low, -other, other) * sine


def unrotate(grads, cosine, sine):
    low, other = swapped(grads * sine)
    return grads * cosine + jnp.where(low, other, -other)


def wide(table):
    return jnp.concatenate([table] * (GROUP // LANES), axis=1)


def head_lanes(values, head):
    lane = lax.broadcasted_iota(jnp.int32, values.shape, 1)
    return jnp.where((lane // HEAD) == head, values, jnp.zeros_like(values))


def pick(first, second):
    lane = lax.broadcasted_iota(jnp.int32, first.shape, 1)
    return jnp.where(lane < HEAD, first, second)


def move_kernel(blocks, *refs):
    parts, table, out = refs[:blocks], refs[blocks], refs[blocks + 1]
    rows = parts[0].shape[0]
    for i in range(blocks):
        out[i * rows : (i + 1) * rows, :] = dot(parts[i][...], table[...]).astype(BF)


def forward_kernel(
    reach, x_ref, gain_ref, cos_ref, sin_ref, bias_ref,
    qa, qb, ka, kb, va, vb,
    q_out, k_out, v_out, attn_out, lse_out, norm_ref,
):
    tok = attn_out.shape[0]
    blocks = x_ref.shape[0] // tok
    scale = HEAD ** (-0.5)

    @pl.when(pl.program_id(0) == 0)
    def _():
        for i in range(blocks):
            rows = pl.ds(i * tok, tok)
            scaled, _, _ = layer_norm(x_ref[rows, :].astype(F32), gain_ref[0:1, :])
            norm_ref[rows, :] = scaled.astype(BF)

    half = norm_ref.shape[1] // 2
    for i in range(blocks):
        rows = pl.ds(i * tok, tok)
        xa, xb = norm_ref[rows, :half], norm_ref[rows, half:]
        cosine, sine = wide(cos_ref[rows, :]), wide(sin_ref[rows, :])
        q_out[rows, :] = rotate(dot(xa, qa[...]) + dot(xb, qb[...]), cosine, sine).astype(BF)
        k_out[rows, :] = rotate(dot(xa, ka[...]) + dot(xb, kb[...]), cosine, sine).astype(BF)
        v_out[rows, :] = (dot(xa, va[...]) + dot(xb, vb[...])).astype(BF)

    bias = bias_ref[...]
    own = pl.ds(reach * tok, tok)
    for pair in range(GROUP // LANES):
        lanes = slice(pair * LANES, (pair + 1) * LANES)
        query, key, value = q_out[own, lanes], k_out[:, lanes], v_out[:, lanes]
        results, logs = [], []
        for head in range(2):
            scores = dot_nt(head_lanes(query, head), key) * scale + bias
            top = jnp.max(scores, axis=-1, keepdims=True)
            weights = jnp.exp(scores - top)
            total = jnp.sum(weights, axis=-1, keepdims=True)
            results.append(dot(weights.astype(BF), value) / total)
            logs.append(jnp.broadcast_to(top + jnp.log(total), (tok, LANES)))
        attn_out[:, lanes] = pick(*results).astype(BF)
        lse_out[:, lanes] = pick(*logs)


def query_kernel(
    q_ref, k_ref, v_ref, g_ref, a_ref, lse_ref, bias_ref, cos_ref, sin_ref, out_ref
):
    scale = HEAD ** (-0.5)
    bias = bias_ref[...]
    cosine, sine = cos_ref[...], sin_ref[...]
    for pair in range(GROUP // LANES):
        lanes = slice(pair * LANES, (pair + 1) * LANES)
        query, key, value = q_ref[:, lanes], k_ref[:, lanes], v_ref[:, lanes]
        grad = g_ref[:, lanes]
        product = grad.astype(F32) * a_ref[:, lanes].astype(F32)
        results = []
        for head in range(2):
            lse = lse_ref[:, pair * LANES + head * HEAD : pair * LANES + head * HEAD + 1]
            delta = jnp.sum(head_lanes(product, head), axis=-1, keepdims=True)
            scores = dot_nt(head_lanes(query, head), key) * scale + bias
            probs = jnp.exp(scores - lse)
            grad_probs = dot_nt(head_lanes(grad, head), value)
            grad_scores = (probs * (grad_probs - delta) * scale).astype(BF)
            results.append(dot(grad_scores, key))
        out_ref[:, lanes] = unrotate(pick(*results), cosine, sine).astype(BF)


def key_kernel(blocks, q_ref, k_ref, v_ref, lse_ref, delta_ref, bias_ref, cos_ref, sin_ref, *refs):
    grads, key_out, value_out = refs[:blocks], refs[blocks], refs[blocks + 1]
    scale = HEAD ** (-0.5)
    bias = bias_ref[...]
    cosine, sine = cos_ref[...], sin_ref[...]
    first = pl.program_id(0) * HEADS_STEP
    for pair in range(GROUP // LANES):
        lanes = slice(pair * LANES, (pair + 1) * LANES)
        query, key, value = q_ref[:, lanes], k_ref[:, lanes], v_ref[:, lanes]
        grad = jnp.concatenate([g[:, lanes] for g in grads], axis=0)
        key_parts, value_parts = [], []
        for head in range(2):
            row = first + (2 * pair + head)
            lse = lse_ref[pl.ds(row, 1), :]
            delta = delta_ref[pl.ds(row, 1), :]
            scores = dot_nt(head_lanes(key, head), query) * scale + bias
            probs = jnp.exp(scores - lse)
            value_parts.append(dot(probs.astype(BF), grad))
            grad_probs = dot_nt(head_lanes(value, head), grad)
            grad_scores = (probs * (grad_probs - delta) * scale).astype(BF)
            key_parts.append(dot(grad_scores, query))
        key_out[:, lanes] = unrotate(pick(*key_parts), cosine, sine).astype(BF)
        value_out[:, lanes] = pick(*value_parts).astype(BF)


def whole(shape):
    return pl.BlockSpec(shape, lambda p: (0,) * len(shape))


def columns(rows, offset=0, row_block=0):
    return pl.BlockSpec((rows, GROUP), lambda p: (row_block, offset + p))


def high_low(values, pieces):
    out = []
    for _ in range(pieces):
        high = lax.reduce_precision(values, 8, 7)
        out.append(high.astype(BF))
        values = values - high
    return out


def local(
    inputs,
    segments,
    positions,
    attention_norm_gain,
    query_key_value_weight,
    attention_output_weight,
    feedforward_norm_gain,
    input_projection_weight,
    down_projection_weight,
    cotangent,
):
    tok, width = inputs.shape
    heads = width // HEAD
    half = width // 2
    rows = query_key_value_weight.shape[0]
    fsdp, ctx = lax.axis_size("fsdp"), lax.axis_size("ctx")
    count = fsdp * ctx
    groups = exchange_groups(fsdp, ctx)
    own_index = lax.axis_index("ctx")
    me = lax.axis_index("fsdp") * ctx + own_index
    reach = -(-LONGEST_DOCUMENT // tok)
    blocks = 2 * reach + 1
    window = blocks * tok
    steps = width // GROUP

    lane_id = jnp.arange(LANES)[None, :]
    gain_cols = jnp.where(
        lane_id == 0, attention_norm_gain[:, None], feedforward_norm_gain[:, None]
    )
    qkv_a, qkv_b = gather_rows(
        jnp.concatenate([query_key_value_weight, gain_cols], axis=1), groups, count
    )
    x_blocks = [inputs if r == 0 else shifted(inputs, -r) for r in range(-reach, reach + 1)]
    rest_a, rest_b = gather_rows(
        jnp.concatenate(
            [attention_output_weight, input_projection_weight, down_projection_weight], axis=1
        ),
        groups,
        count,
    )

    masks = jnp.asarray(slot_masks(groups), jnp.int32)
    source = ((me ^ masks)[:, None] * rows + jnp.arange(rows)[None, :]).reshape(-1)
    to_rel = (jnp.arange(width)[:, None] == source[None, :]).astype(BF)
    to_nat = (source[:, None] == jnp.arange(width)[None, :]).astype(BF)

    row_segs = segments[0]
    pad = reach * tok
    low_pad = jnp.full((pad,), -1, jnp.int32)
    high_pad = jnp.full((pad,), jnp.iinfo(jnp.int32).max, jnp.int32)
    window_segs = lax.dynamic_slice_in_dim(
        jnp.concatenate([low_pad, row_segs, high_pad]), own_index * tok, window
    )
    own_segs = window_segs[pad : pad + tok]
    before = jnp.sum((window_segs[None, :] < window_segs[:, None]).astype(jnp.int32), axis=1)
    cosine, sine = rope_tables(jnp.arange(window) - before)
    bias = jnp.where(own_segs[:, None] == window_segs[None, :], 0.0, NEG).astype(F32)

    cot_rel = dot(cotangent, to_rel).astype(BF)
    x_rel = pl.pallas_call(
        functools.partial(move_kernel, blocks),
        out_shape=jax.ShapeDtypeStruct((window, width), BF),
        name="move_inputs",
    )(*x_blocks, to_rel)

    gain_table = jnp.concatenate([qkv_a[:, 3 * width :], qkv_b[:, 3 * width :]], axis=0)
    select = (jnp.arange(8)[:, None] == jnp.arange(LANES)[None, :]).astype(BF)
    gains = dot_nt(select, gain_table)
    attn_gain, mlp_gain = gains[0:1], gains[1:2]

    window_cols = jax.ShapeDtypeStruct((window, width), BF)
    q_win, k_win, v_win, attn, lse = pl.pallas_call(
        functools.partial(forward_kernel, reach),
        grid=(steps,),
        in_specs=[
            whole((window, width)),
            whole((8, width)),
            whole((window, LANES)),
            whole((window, LANES)),
            whole((tok, window)),
            columns(half),
            columns(half),
            columns(half, steps),
            columns(half, steps),
            columns(half, 2 * steps),
            columns(half, 2 * steps),
        ],
        out_specs=[columns(window)] * 3 + [columns(tok)] * 2,
        out_shape=[window_cols] * 3
        + [jax.ShapeDtypeStruct((tok, width), BF), jax.ShapeDtypeStruct((tok, width), F32)],
        scratch_shapes=[pltpu.VMEM((window, width), BF)],
        name="attention_forward",
    )(x_rel, gains, cosine, sine, bias, qkv_a, qkv_b, qkv_a, qkv_b, qkv_a, qkv_b)

    out_rows = dot(to_rel[:, :half], rest_a[:, :width]) + dot(to_rel[:, half:], rest_b[:, :width])
    out_weight = dot(out_rows.astype(BF), to_rel).astype(BF)
    in_a, in_b = rest_a[:, width : width + 2 * FF], rest_b[:, width : width + 2 * FF]
    down_a, down_b = rest_a[:, width + 2 * FF :], rest_b[:, width + 2 * FF :]

    x_own = x_rel[pad : pad + tok].astype(F32)
    resid = x_own + dot(attn, out_weight)
    mlp_scaled, mlp_normed, mlp_inv = layer_norm(resid, mlp_gain)
    mlp_input = mlp_scaled.astype(BF)
    up_rows = dot(mlp_input[:, :half], in_a) + dot(mlp_input[:, half:], in_b)
    gate_in, gate_mul = up_rows[:, :FF], up_rows[:, FF:]
    gelu_value, gelu_slope = gelu_parts(gate_in)
    hidden = (gelu_value * gate_mul).astype(BF)
    grad_hidden = dot(cot_rel[:, :half], down_a) + dot(cot_rel[:, half:], down_b)
    grad_up = jnp.concatenate(
        [grad_hidden * gate_mul * gelu_slope, grad_hidden * gelu_value], axis=1
    ).astype(BF)
    grad_mlp_input = jnp.concatenate([dot_nt(grad_up, in_a), dot_nt(grad_up, in_b)], axis=1)
    grad_resid = cot_rel.astype(F32) + norm_back(grad_mlp_input, mlp_normed, mlp_inv, mlp_gain)
    grad_low = grad_resid.astype(BF)
    grad_attn = dot_nt(grad_low, out_weight).astype(BF)

    member = (jnp.arange(width)[:, None] // HEAD == jnp.arange(LANES)[None, :]).astype(F32)
    delta = jnp.dot(
        grad_attn.astype(F32) * attn.astype(F32), member, precision=lax.Precision.HIGHEST
    )[:, :heads]
    lse_cols = lse.reshape(tok, heads, HEAD)[:, :, 0]
    stats = high_low(lse_cols, 3) + high_low(delta, 2)
    filler = jnp.zeros((tok, LANES - 5 * heads), BF)
    message = jnp.concatenate([grad_attn] + stats + [filler], axis=1)
    messages = [message if r == 0 else shifted(message, -r) for r in range(-reach, reach + 1)]

    own_cols = columns(tok, 0, reach)
    table_own = pl.BlockSpec((tok, LANES), lambda p: (reach, 0))
    grad_query = pl.pallas_call(
        query_kernel,
        grid=(steps,),
        in_specs=[
            own_cols,
            columns(window),
            columns(window),
            columns(tok),
            columns(tok),
            columns(tok),
            whole((tok, window)),
            pl.BlockSpec((tok, LANES), lambda p: (reach, 0)),
            table_own,
        ],
        out_specs=columns(tok),
        out_shape=jax.ShapeDtypeStruct((tok, width), BF),
        name="attention_query_grad",
    )(q_win, k_win, v_win, grad_attn, attn, lse, bias, cosine, sine)

    attn_rel = dot(attn, to_rel).astype(BF)
    grad_low_nat = dot(grad_low, to_nat).astype(BF)
    ones = jnp.ones((tok, LANES), BF)
    mlp_gain_terms = (grad_mlp_input * mlp_normed).astype(BF)

    def rest_half(cut):
        return jnp.concatenate(
            [
                dot_tn(attn_rel[:, cut], grad_low_nat),
                dot_tn(mlp_input[:, cut], grad_up),
                dot_tn(cot_rel[:, cut], hidden),
                dot_tn(mlp_gain_terms[:, cut], ones),
            ],
            axis=1,
        )

    first, second = slice(0, half), slice(half, width)
    rest_part = scatter_rows(rest_half(first), rest_half(second).astype(BF), groups, count)

    down_rel = jnp.concatenate([dot_nt(hidden, down_a), dot_nt(hidden, down_b)], axis=1)
    outputs = dot((resid + down_rel).astype(BF), to_nat).astype(BF)

    stat_rows = jnp.concatenate([m[:, width:] for m in messages], axis=0).astype(F32)
    lse_win = (
        stat_rows[:, :heads] + stat_rows[:, heads : 2 * heads] + stat_rows[:, 2 * heads : 3 * heads]
    )
    delta_win = stat_rows[:, 3 * heads : 4 * heads] + stat_rows[:, 4 * heads : 5 * heads]
    grad_key, grad_value = pl.pallas_call(
        functools.partial(key_kernel, blocks),
        grid=(steps,),
        in_specs=[
            columns(window),
            own_cols,
            own_cols,
            whole((heads, window)),
            whole((heads, window)),
            whole((tok, window)),
            table_own,
            table_own,
        ]
        + [columns(tok)] * blocks,
        out_specs=[columns(tok)] * 2,
        out_shape=[jax.ShapeDtypeStruct((tok, width), BF)] * 2,
        name="attention_key_grad",
    )(q_win, k_win, v_win, lse_win.T, delta_win.T, bias, cosine, sine, *messages)

    grad_qkv = jnp.concatenate([grad_query, grad_key, grad_value], axis=1)
    grad_attn_input = jnp.concatenate(
        [dot_nt(grad_qkv, qkv_a[:, : 3 * width]), dot_nt(grad_qkv, qkv_b[:, : 3 * width])], axis=1
    )
    attn_scaled, attn_normed, attn_inv = layer_norm(x_own, attn_gain)
    attn_input = attn_scaled.astype(BF)
    attn_gain_terms = (grad_attn_input * attn_normed).astype(BF)

    def qkv_half(cut):
        return jnp.concatenate(
            [dot_tn(attn_input[:, cut], grad_qkv), dot_tn(attn_gain_terms[:, cut], ones)], axis=1
        )

    qkv_part = scatter_rows(qkv_half(first), qkv_half(second).astype(BF), groups, count)
    grad_x = norm_back(grad_attn_input, attn_normed, attn_inv, attn_gain)
    input_grad = dot((grad_resid + grad_x).astype(BF), to_nat).astype(BF)

    return (
        outputs,
        input_grad,
        qkv_part[:, 3 * width],
        qkv_part[:, : 3 * width],
        rest_part[:, :width],
        rest_part[:, 3 * FF + width],
        rest_part[:, width : width + 2 * FF],
        rest_part[:, width + 2 * FF : width + 3 * FF],
    )


def solution(mesh):
    in_specs = (
        P(("fsdp", "ctx"), None),
        P("fsdp", None),
        P("fsdp", "ctx"),
        P(("fsdp", "ctx")),
        P(("fsdp", "ctx"), None),
        P(("fsdp", "ctx"), None),
        P(("fsdp", "ctx")),
        P(("fsdp", "ctx"), None),
        P(("fsdp", "ctx"), None),
        P(("fsdp", "ctx"), None),
    )
    out_specs = (
        P(("fsdp", "ctx"), None),
        P(("fsdp", "ctx"), None),
        P(("fsdp", "ctx")),
        P(("fsdp", "ctx"), None),
        P(("fsdp", "ctx"), None),
        P(("fsdp", "ctx")),
        P(("fsdp", "ctx"), None),
        P(("fsdp", "ctx"), None),
    )
    return jax.shard_map(local, mesh=mesh, in_specs=in_specs, out_specs=out_specs, check_vma=False)
```

time: 759 us -> 337 us (0.44)
  waiting for transfers between devices: 464 us -> 140 us
  blocking collectives: 82.3 us -> 0 us
  Pallas kernels: 0 us -> 33.6 us
  local copies, waits for them, and re-layouts: 45.8 us -> 22.1 us
  matrix products: 67.7 us -> 44.6 us
  between operations: 15.1 us -> 1.76 us
  starting transfers between devices: 62 us -> 71 us
    reduce_scatter x3 -> x0, waiting for transfers between devices: 344 us -> none  [the longest x1 125 us: local(): lax.psum_scatter(in_grad, ('fsdp', 'ctx'), scatter_dimension=0, tiled=True)]
    ppermute x24 -> x40, waiting for transfers between devices: 36.3 us -> 140 us  [the longest x28 119 us: xor_permute(): return lax.ppermute(value, AXES, [(d, d ^ mask) for d in range(count)])]
    unnamed x2 -> x0, blocking collectives: 82.3 us -> none
    all_gather x4 -> x0, waiting for transfers between devices: 81.4 us -> none  [the longest x1 51.6 us: local(): lax.all_gather(down_projection_weight, ('fsdp', 'ctx'), axis=0, tiled=True)]
    pallas_call x0 -> x4, Pallas kernels: none -> 33.6 us  [the longest x1 14.2 us: local(): pl.pallas_call(functools.partial(forward_kernel, reach), grid=(steps,), i...]
    dot_general x61 -> x33, matrix products: 67.7 us -> 44.6 us  [the longest x12 22.7 us: dot(): return jnp.dot(a, b, preferred_element_type=F32)]
    unnamed x82 -> x107, local copies, waits for them, and re-layouts: 21.5 us -> 10.4 us
    dynamic_slice x15 -> x0, local copies, waits for them, and re-layouts: 10.1 us -> none  [the longest x14 9.54 us: local(): lax.scan(forward_step, (start_max, start_sum, start_acc), (key_blocks, va...]
  transfers between devices with their start and end apart: 32 -> 40, of which waited for: 13 -> 18; matrix products, arithmetic and copies ran while one was open for 17% -> 18% of each run, Pallas kernels for 0% -> 10%
where the time goes in v1:
time: 337 us; the launch traced here: 335 us
  waiting for transfers between devices  140 us (42%)
  starting transfers between devices  71 us (21%)
  matrix products  44.6 us (13%)
  Pallas kernels  33.6 us (10%)
  local copies, waits for them, and re-layouts  22.1 us (7%)
  other arithmetic  21.8 us (6%)
    ppermute x28, waiting for transfers between devices, xor_permute(): return lax.ppermute(value, AXES, [(d, d ^ mask) for d in range(count)])  119 us
    ppermute x28, starting transfers between devices, xor_permute(): return lax.ppermute(value, AXES, [(d, d ^ mask) for d in range(count)])  43.7 us
    ppermute x12, starting transfers between devices, shifted(): lax.ppermute(value, 'ctx', [(s, s + steps) for s in range(first, last)])  27.4 us
    dot_general x12, matrix products, dot(): return jnp.dot(a, b, preferred_element_type=F32)  22.7 us
    ppermute x12, waiting for transfers between devices, shifted(): lax.ppermute(value, 'ctx', [(s, s + steps) for s in range(first, last)])  21 us
    pallas_call x1, Pallas kernels, local(): pl.pallas_call(functools.partial(forward_kernel, reach), grid=(steps,), i...  14.2 us
    dot_general x8, matrix products, dot_nt(): lax.dot_general(a, b, (((1,), (1,)), ((), ())), preferred_element_type=F32)  14.1 us
    unnamed x107, local copies, waits for them, and re-layouts  10.4 us
  transfers between devices with their start and end apart: 40, of which 18 were waited for; matrix products, arithmetic and copies ran while one was open for 18% of the time, Pallas kernels for 10%

profile of v1, /device:TPU:0, one launch (start us, length us, event | category | flops | bytes accessed | tf_op | source)
XLA Modules:
  0.0 335.2 jit_solution(14279830489237488386)
XLA Ops:
  0.7 4.5 %collective-permute-start = (bf16[128,768]{1,0:T(8,128)(2,1)}, bf16[128,768]{1,0:T(8,128)(2,1)S(1)}, u32[]{:S(2)}, u32[]{:S(2)}) collective-permute-start(bf16[128,768]{1,0:T(8,128)(2,1)} %refs_3_.1), channel_id=1, source_target_pairs={{0,3},{1,4},{2,5},{3,6},{4,7},{8,11},{9,12},{10,13},{11,14},{12,15... | collective-permute-start | bytes 589832 | tf_op jit(solution)/shard_map/ppermute | solution.py:75
  5.2 3.5 %collective-permute-start.1 = (bf16[128,768]{1,0:T(8,128)(2,1)}, bf16[128,768]{1,0:T(8,128)(2,1)S(1)}, u32[]{:S(2)}, u32[]{:S(2)}) collective-permute-start(bf16[128,768]{1,0:T(8,128)(2,1)} %refs_3_.1), channel_id=1, source_target_pairs={{0,2},{1,3},{2,4},{3,5},{4,6},{5,7},{8,10},{9,11},{10,12},{11,13},... | collective-permute-start | bytes 589832 | tf_op jit(solution)/shard_map/ppermute | solution.py:75
  12.0 2.8 collective-permute-start.8
  24.0 4.1 %collective-permute-start.15 = (bf16[24,4224]{1,0:T(8,128)(2,1)S(1)}, bf16[24,4224]{1,0:T(8,128)(2,1)S(1)}, u32[]{:S(2)}, u32[]{:S(2)}) collective-permute-start(bf16[24,4224]{1,0:T(8,128)(2,1)S(1)} %get-tuple-element.65), channel_id=1, source_target_pairs={{0,6},{1,7},{2,4},{3,5},{4,2},{5,3},{6,0},{7,1},{8,14},{9,15},{10,... | collective-permute-start | bytes 608264 | tf_op jit(solution)/shard_map/ppermute | solution.py:47
  29.0 3.2 collective-permute-done.13
  33.9 5.4 %collective-permute-done.14 = bf16[24,4224]{1,0:T(8,128)(2,1)S(1)} collective-permute-done((bf16[24,4224]{1,0:T(8,128)(2,1)S(1)}, bf16[24,4224]{1,0:T(8,128)(2,1)S(1)}, u32[]{:S(2)}, u32[]{:S(2)}) %collective-permute-start.14) | collective-permute-done | bytes 202784 | tf_op jit(solution)/shard_map/ppermute | solution.py:47
  43.6 9.3 %collective-permute-done.9 = bf16[96,2432]{1,0:T(8,128)(2,1)S(1)} collective-permute-done((bf16[96,2432]{1,0:T(8,128)(2,1)S(1)}, bf16[96,2432]{1,0:T(8,128)(2,1)S(1)}, u32[]{:S(2)}, u32[]{:S(2)}) %collective-permute-start.9) | collective-permute-done | bytes 466976 | tf_op jit(solution)/shard_map/ppermute | solution.py:47
  54.4 12.2 %collective-permute-done.16 = bf16[96,4224]{1,0:T(8,128)(2,1)S(1)} collective-permute-done((bf16[96,4224]{1,0:T(8,128)(2,1)S(1)}, bf16[96,4224]{1,0:T(8,128)(2,1)S(1)}, u32[]{:S(2)}, u32[]{:S(2)}) %collective-permute-start.16) | collective-permute-done | bytes 811040 | tf_op jit(solution)/shard_map/ppermute | solution.py:47
  66.6 3.5 %collective-permute-start.18 = (bf16[96,4224]{1,0:T(8,128)(2,1)S(1)}, bf16[96,4224]{1,0:T(8,128)(2,1)S(1)}, u32[]{:S(2)}, u32[]{:S(2)}) collective-permute-start(bf16[96,4224]{1,0:T(8,128)(2,1)S(1)} %pad_maximum_fusion.2), channel_id=1, source_target_pairs={{0,24},{1,25},{2,26},{3,27},{4,28},{5,29},{6,30},{7,31},{8,16},{9,... | collective-permute-start | bytes 2433032 | tf_op jit(solution)/shard_map/ppermute | solution.py:47
  71.0 19.3 %collective-permute-done.17 = bf16[96,4224]{1,0:T(8,128)(2,1)S(1)} collective-permute-done((bf16[96,4224]{1,0:T(8,128)(2,1)S(1)}, bf16[96,4224]{1,0:T(8,128)(2,1)S(1)}, u32[]{:S(2)}, u32[]{:S(2)}) %collective-permute-start.17) | collective-permute-done | bytes 811040 | tf_op jit(solution)/shard_map/ppermute | solution.py:47
  95.8 8.1 %collective-permute-done.10 = bf16[96,2432]{1,0:T(8,128)(2,1)S(1)} collective-permute-done((bf16[96,2432]{1,0:T(8,128)(2,1)S(1)}, bf16[96,2432]{1,0:T(8,128)(2,1)S(1)}, u32[]{:S(2)}, u32[]{:S(2)}) %collective-permute-start.10) | collective-permute-done | bytes 466976 | tf_op jit(solution)/shard_map/ppermute | solution.py:47
  104.6 2.6 multiply_sine_fusion
  114.9 13.6 %collective-permute-done.4.refs_5_ = bf16[128,768]{1,0:T(8,128)(2,1)S(1)} collective-permute-done((bf16[128,768]{1,0:T(8,128)(2,1)S(1)}, bf16[128,768]{1,0:T(8,128)(2,1)S(1)}, u32[]{:S(2)}, u32[]{:S(2)}) %collective-permute-start.4) | collective-permute-done | bytes 196640 | tf_op jit(solution)/shard_map/ppermute | solution.py:75
  128.4 2.5 collective-permute-done.5.refs_6_
  131.6 4.2 %move_inputs.1.x_ref = bf16[896,768]{1,0:T(8,128)(2,1)} custom-call(bf16[128,768]{1,0:T(8,128)(2,1)} %copy-done.29, bf16[128,768]{1,0:T(8,128)(2,1)} %copy-done.30, bf16[128,768]{1,0:T(8,128)(2,1)} %copy-done.31, bf16[128,768]{1,0:T(8,128)(2,1)} %refs_3_.1, bf16[128,768]{1,0:T(8,128)(2,1)} %copy-done.32, bf16[128,768]{1,0:T(8,128)(2,1)} %copy-done.33, ...), custom_call_target="tpu_custom_call" | custom-call | tf_op jit(solution)/shard_map/move_inputs/pallas_call | solution.py:331
  140.2 14.2 %attention_forward.1 = (bf16[896,768]{1,0:T(8,128)(2,1)}, bf16[896,768]{1,0:T(8,128)(2,1)}, bf16[896,768]{1,0:T(8,128)(2,1)}, bf16[128,768]{1,0:T(8,128)(2,1)}, f32[128,768]{1,0:T(8,128)}) custom-call(bf16[896,768]{1,0:T(8,128)(2,1)} %move_inputs.1.x_ref, f32[8,768]{1,0:T(8,128)} %fusion.85.gain_ref, f32[896,128]{1,0:T(8,128)} %get-tuple-element.70.cos_ref, ...), custom_call_target="tpu_custom_call" | custom-call | tf_op jit(solution)/shard_map/attention_forward/pallas_call | solution.py:343
  159.4 3.4 %fusion.27 = f32[768,768]{1,0:T(8,128)} fusion(pred[768,768]{1,0:T(32,128)(4,1)S(1)} %get-tuple-element.71, bf16[384,4224]{1,0:T(8,128)(2,1)} %collective-permute-done.19), kind=kOutput, calls=%fused_computation.43 | convolution fusion | flops 452984832 | bytes 3244032 | tf_op jit(solution)/shard_map/dot_general | solution.py:79
  162.8 3.8 %fusion.20 = bf16[768,768]{1,0:T(8,128)(2,1)S(1)} fusion(s32[768]{0:T(1024)S(1)} %add.147, f32[768,768]{1,0:T(8,128)} %fusion.27, pred[768,768]{1,0:T(32,128)(4,1)S(1)} %get-tuple-element.71, bf16[384,4224]{1,0:T(8,128)(2,1)} %constant_dynamic-update-slice_fusion.10), kind=kOutput, calls=%fused_computation.34 | convolution fusion | flops 1361313792 | bytes 4427776 | tf_op jit(solution)/shard_map/dot_general | solution.py:79
  182.2 5.8 %collective-permute-start.20 = (bf16[128,896]{1,0:T(8,128)(2,1)S(1)}, bf16[128,896]{1,0:T(8,128)(2,1)S(1)}, u32[]{:S(2)}, u32[]{:S(2)}) collective-permute-start(bf16[128,896]{1,0:T(8,128)(2,1)S(1)} %concatenate.76.refs_3_), channel_id=1, source_target_pairs={{0,3},{1,4},{2,5},{3,6},{4,7},{8,11},{9,12},{10,13},{11,14},{12,15... | collective-permute-start | bytes 688136 | tf_op jit(solution)/shard_map/ppermute | solution.py:75
  206.9 6.8 %attention_query_grad.1 = bf16[128,768]{1,0:T(8,128)(2,1)} custom-call(bf16[896,768]{1,0:T(8,128)(2,1)} %get-tuple-element.16.q_ref, bf16[896,768]{1,0:T(8,128)(2,1)} %get-tuple-element.17.k_ref, bf16[896,768]{1,0:T(8,128)(2,1)} %get-tuple-element.18.v_ref, bf16[128,768]{1,0:T(8,128)(2,1)} %copy-done.7, bf16[128,768]{1,0:T(8,128)(2,1)} %get-tuple-element.15.a_ref, ...), custom_call_target="tpu_custom_call" | custom-call | tf_op jit(solution)/shard_map/attention_query_grad/pallas_call | solution.py:400
  218.2 4.9 %collective-permute-done.25.refs_6_ = bf16[128,896]{1,0:T(8,128)(2,1)S(1)} collective-permute-done((bf16[128,896]{1,0:T(8,128)(2,1)S(1)}, bf16[128,896]{1,0:T(8,128)(2,1)S(1)}, u32[]{:S(2)}, u32[]{:S(2)}) %collective-permute-start.25) | collective-permute-done | bytes 229408 | tf_op jit(solution)/shard_map/ppermute | solution.py:75
  225.5 8.4 %attention_key_grad.1 = (bf16[128,768]{1,0:T(8,128)(2,1)}, bf16[128,768]{1,0:T(8,128)(2,1)}) custom-call(bf16[896,768]{1,0:T(8,128)(2,1)} %get-tuple-element.16.q_ref, bf16[896,768]{1,0:T(8,128)(2,1)} %get-tuple-element.17.k_ref, bf16[896,768]{1,0:T(8,128)(2,1)} %get-tuple-element.18.v_ref, f32[12,896]{1,0:T(8,128)} %copy.50.lse_ref, ...), custom_call_target="tpu_custom_call" | custom-call | tf_op jit(solution)/shard_map/attention_key_grad/pallas_call | solution.py:446
  240.1 5.9 %collective-permute-start.26 = (bf16[384,2432]{1,0:T(8,128)(2,1)S(1)}, bf16[384,2432]{1,0:T(8,128)(2,1)S(1)}, u32[]{:S(2)}, u32[]{:S(2)}) collective-permute-start(bf16[384,2432]{1,0:T(8,128)(2,1)S(1)} %pad_maximum_fusion.1), channel_id=1, source_target_pairs={{0,1},{1,0},{2,3},{3,2},{4,5},{5,4},{6,7},{7,6},{8,9},{9,8},{10,11... | collective-permute-start | bytes 5603336 | tf_op jit(solution)/shard_map/ppermute | solution.py:47
  252.0 2.5 collective-permute-start.29
  258.0 2.5 collective-permute-start.36
  261.1 5.5 %collective-permute-done.29 = bf16[96,2432]{1,0:T(8,128)(2,1)S(1)} collective-permute-done((bf16[96,2432]{1,0:T(8,128)(2,1)S(1)}, bf16[96,2432]{1,0:T(8,128)(2,1)S(1)}, u32[]{:S(2)}, u32[]{:S(2)}) %collective-permute-start.29) | collective-permute-done | bytes 466976 | tf_op jit(solution)/shard_map/ppermute | solution.py:47
  268.0 8.5 %collective-permute-done.28 = bf16[96,2432]{1,0:T(8,128)(2,1)S(1)} collective-permute-done((bf16[96,2432]{1,0:T(8,128)(2,1)S(1)}, bf16[96,2432]{1,0:T(8,128)(2,1)S(1)}, u32[]{:S(2)}, u32[]{:S(2)}) %collective-permute-start.28) | collective-permute-done | bytes 466976 | tf_op jit(solution)/shard_map/ppermute | solution.py:47
  279.4 15.1 %collective-permute-done.36 = bf16[96,4352]{1,0:T(8,128)(2,1)S(1)} collective-permute-done((bf16[96,4352]{1,0:T(8,128)(2,1)S(1)}, bf16[96,4352]{1,0:T(8,128)(2,1)S(1)}, u32[]{:S(2)}, u32[]{:S(2)}) %collective-permute-start.36) | collective-permute-done | bytes 835616 | tf_op jit(solution)/shard_map/ppermute | solution.py:47
  295.4 16.7 %collective-permute-done.35 = bf16[96,4352]{1,0:T(8,128)(2,1)S(1)} collective-permute-done((bf16[96,4352]{1,0:T(8,128)(2,1)S(1)}, bf16[96,4352]{1,0:T(8,128)(2,1)S(1)}, u32[]{:S(2)}, u32[]{:S(2)}) %collective-permute-start.35) | collective-permute-done | bytes 835616 | tf_op jit(solution)/shard_map/ppermute | solution.py:47
  314.1 3.0 collective-permute-start.37
  318.5 4.1 %collective-permute-done.39 = bf16[24,4352]{1,0:T(8,128)(2,1)S(1)} collective-permute-done((bf16[24,4352]{1,0:T(8,128)(2,1)S(1)}, bf16[24,4352]{1,0:T(8,128)(2,1)S(1)}, u32[]{:S(2)}, u32[]{:S(2)}) %collective-permute-start.39) | collective-permute-done | bytes 208928 | tf_op jit(solution)/shard_map/ppermute | solution.py:47
  322.7 9.8 %collective-permute-done.38 = bf16[24,4352]{1,0:T(8,128)(2,1)S(1)} collective-permute-done((bf16[24,4352]{1,0:T(8,128)(2,1)S(1)}, bf16[24,4352]{1,0:T(8,128)(2,1)S(1)}, u32[]{:S(2)}, u32[]{:S(2)}) %collective-permute-start.38) | collective-permute-done | bytes 208928 | tf_op jit(solution)/shard_map/ppermute | solution.py:47
  (260 shorter events, 113.6 us)
Async XLA Ops:
  0.7 109.0 %collective-permute-start = (bf16[128,768]{1,0:T(8,128)(2,1)}, bf16[128,768]{1,0:T(8,128)(2,1)S(1)}, u32[]{:S(2)}, u32[]{:S(2)}) collective-permute-start(bf16[128,768]{1,0:T(8,128)(2,1)} %refs_3_.1), channel_id=1, source_target_pairs={{0,3},{1,4},{2,5},{3,6},{4,7},{8,11},{9,12},{10,13},{11,14},{12,15... | collective-permute-start | bytes 589832 | tf_op jit(solution)/shard_map/ppermute | solution.py:75
  5.2 105.8 %collective-permute-start.1 = (bf16[128,768]{1,0:T(8,128)(2,1)}, bf16[128,768]{1,0:T(8,128)(2,1)S(1)}, u32[]{:S(2)}, u32[]{:S(2)}) collective-permute-start(bf16[128,768]{1,0:T(8,128)(2,1)} %refs_3_.1), channel_id=1, source_target_pairs={{0,2},{1,3},{2,4},{3,5},{4,6},{5,7},{8,10},{9,11},{10,12},{11,13},... | collective-permute-start | bytes 589832 | tf_op jit(solution)/shard_map/ppermute | solution.py:75
  12.0 11.9 %collective-permute-start.8 = (bf16[24,2432]{1,0:T(8,128)(2,1)S(1)}, bf16[24,2432]{1,0:T(8,128)(2,1)S(1)}, u32[]{:S(2)}, u32[]{:S(2)}) collective-permute-start(bf16[24,2432]{1,0:T(8,128)(2,1)S(1)} %get-tuple-element.56), channel_id=1, source_target_pairs={{0,6},{1,7},{2,4},{3,5},{4,2},{5,3},{6,0},{7,1},{8,14},{9,15},{10,... | collective-permute-start | bytes 350216 | tf_op jit(solution)/shard_map/ppermute | solution.py:47
  23.9 15.4 %collective-permute-start.14 = (bf16[24,4224]{1,0:T(8,128)(2,1)S(1)}, bf16[24,4224]{1,0:T(8,128)(2,1)S(1)}, u32[]{:S(2)}, u32[]{:S(2)}) collective-permute-start(bf16[24,4224]{1,0:T(8,128)(2,1)S(1)} %get-tuple-element.65), channel_id=1, source_target_pairs={{0,4},{1,5},{2,6},{3,7},{4,0},{5,1},{6,2},{7,3},{8,12},{9,13},{10,... | collective-permute-start | bytes 608264 | tf_op jit(solution)/shard_map/ppermute | solution.py:47
  24.0 16.8 %collective-permute-start.15 = (bf16[24,4224]{1,0:T(8,128)(2,1)S(1)}, bf16[24,4224]{1,0:T(8,128)(2,1)S(1)}, u32[]{:S(2)}, u32[]{:S(2)}) collective-permute-start(bf16[24,4224]{1,0:T(8,128)(2,1)S(1)} %get-tuple-element.65), channel_id=1, source_target_pairs={{0,6},{1,7},{2,4},{3,5},{4,2},{5,3},{6,0},{7,1},{8,14},{9,15},{10,... | collective-permute-start | bytes 608264 | tf_op jit(solution)/shard_map/ppermute | solution.py:47
  32.2 80.0 %collective-permute-start.2 = (bf16[128,768]{1,0:T(8,128)(2,1)S(1)}, bf16[128,768]{1,0:T(8,128)(2,1)S(1)}, u32[]{:S(2)}, u32[]{:S(2)}) collective-permute-start(bf16[128,768]{1,0:T(8,128)(2,1)S(1)} %copy-done.28), channel_id=1, source_target_pairs={{0,1},{1,2},{2,3},{3,4},{4,5},{5,6},{6,7},{8,9},{9,10},{10,11},{11... | collective-permute-start | bytes 589832 | tf_op jit(solution)/shard_map/ppermute | solution.py:75
  39.3 13.6 %collective-permute-start.9 = (bf16[96,2432]{1,0:T(8,128)(2,1)S(1)}, bf16[96,2432]{1,0:T(8,128)(2,1)S(1)}, u32[]{:S(2)}, u32[]{:S(2)}) collective-permute-start(bf16[96,2432]{1,0:T(8,128)(2,1)S(1)} %pad_maximum_fusion.5), channel_id=1, source_target_pairs={{0,8},{1,9},{2,10},{3,11},{4,12},{5,13},{6,14},{7,15},{8,0},{9,1},... | collective-permute-start | bytes 1400840 | tf_op jit(solution)/shard_map/ppermute | solution.py:47
  40.9 25.7 %collective-permute-start.16 = (bf16[96,4224]{1,0:T(8,128)(2,1)S(1)}, bf16[96,4224]{1,0:T(8,128)(2,1)S(1)}, u32[]{:S(2)}, u32[]{:S(2)}) collective-permute-start(bf16[96,4224]{1,0:T(8,128)(2,1)S(1)} %pad_maximum_fusion.2), channel_id=1, source_target_pairs={{0,8},{1,9},{2,10},{3,11},{4,12},{5,13},{6,14},{7,15},{8,0},{9,1},... | collective-permute-start | bytes 2433032 | tf_op jit(solution)/shard_map/ppermute | solution.py:47
  52.9 37.5 %collective-permute-start.17 = (bf16[96,4224]{1,0:T(8,128)(2,1)S(1)}, bf16[96,4224]{1,0:T(8,128)(2,1)S(1)}, u32[]{:S(2)}, u32[]{:S(2)}) collective-permute-start(bf16[96,4224]{1,0:T(8,128)(2,1)S(1)} %pad_maximum_fusion.2), channel_id=1, source_target_pairs={{0,16},{1,17},{2,18},{3,19},{4,20},{5,21},{6,22},{7,23},{8,24},{9,... | collective-permute-start | bytes 2433032 | tf_op jit(solution)/shard_map/ppermute | solution.py:47
  66.6 26.8 %collective-permute-start.18 = (bf16[96,4224]{1,0:T(8,128)(2,1)S(1)}, bf16[96,4224]{1,0:T(8,128)(2,1)S(1)}, u32[]{:S(2)}, u32[]{:S(2)}) collective-permute-start(bf16[96,4224]{1,0:T(8,128)(2,1)S(1)} %pad_maximum_fusion.2), channel_id=1, source_target_pairs={{0,24},{1,25},{2,26},{3,27},{4,28},{5,29},{6,30},{7,31},{8,16},{9,... | collective-permute-start | bytes 2433032 | tf_op jit(solution)/shard_map/ppermute | solution.py:47
  90.3 13.6 %collective-permute-start.10 = (bf16[96,2432]{1,0:T(8,128)(2,1)S(1)}, bf16[96,2432]{1,0:T(8,128)(2,1)S(1)}, u32[]{:S(2)}, u32[]{:S(2)}) collective-permute-start(bf16[96,2432]{1,0:T(8,128)(2,1)S(1)} %pad_maximum_fusion.5), channel_id=1, source_target_pairs={{0,16},{1,17},{2,18},{3,19},{4,20},{5,21},{6,22},{7,23},{8,24},{9,... | collective-permute-start | bytes 1400840 | tf_op jit(solution)/shard_map/ppermute | solution.py:47
  103.9 55.5 %collective-permute-start.19 = (bf16[384,4224]{1,0:T(8,128)(2,1)}, bf16[384,4224]{1,0:T(8,128)(2,1)}, u32[]{:S(2)}, u32[]{:S(2)}) collective-permute-start(bf16[384,4224]{1,0:T(8,128)(2,1)} %constant_dynamic-update-slice_fusion.10), channel_id=1, source_target_pairs={{0,1},{1,0},{2,3},{3,2},{4,5},{5,4},{6,7},{7,6},{8,9},{9,8},{10,11... | collective-permute-start | bytes 9732104 | tf_op jit(solution)/shard_map/ppermute | solution.py:47
  104.0 34.5 %collective-permute-start.12 = (bf16[384,2432]{1,0:T(8,128)(2,1)S(1)}, bf16[384,2432]{1,0:T(8,128)(2,1)}, u32[]{:S(2)}, u32[]{:S(2)}) collective-permute-start(bf16[384,2432]{1,0:T(8,128)(2,1)S(1)} %constant_dynamic-update-slice_fusion.qa.ka.va), channel_id=1, source_target_pairs={{0,1},{1,0},{2,3},{3,2},{4,5},{5,4},{6,7},{7,6},{8,9},{9,8},{10,11... | collective-permute-start | bytes 5603336 | tf_op jit(solution)/shard_map/ppermute | solution.py:47
  111.0 17.4 %collective-permute-start.4 = (bf16[128,768]{1,0:T(8,128)(2,1)S(1)}, bf16[128,768]{1,0:T(8,128)(2,1)S(1)}, u32[]{:S(2)}, u32[]{:S(2)}) collective-permute-start(bf16[128,768]{1,0:T(8,128)(2,1)S(1)} %copy-done.28), channel_id=1, source_target_pairs={{2,0},{3,1},{4,2},{5,3},{6,4},{7,5},{10,8},{11,9},{12,10},{13,11},... | collective-permute-start | bytes 589832 | tf_op jit(solution)/shard_map/ppermute | solution.py:75
  113.0 17.9 %collective-permute-start.5 = (bf16[128,768]{1,0:T(8,128)(2,1)S(1)}, bf16[128,768]{1,0:T(8,128)(2,1)S(1)}, u32[]{:S(2)}, u32[]{:S(2)}) collective-permute-start(bf16[128,768]{1,0:T(8,128)(2,1)S(1)} %copy-done.28), channel_id=1, source_target_pairs={{3,0},{4,1},{5,2},{6,3},{7,4},{11,8},{12,9},{13,10},{14,11},{15,12... | collective-permute-start | bytes 589832 | tf_op jit(solution)/shard_map/ppermute | solution.py:75
  182.2 31.6 %collective-permute-start.20 = (bf16[128,896]{1,0:T(8,128)(2,1)S(1)}, bf16[128,896]{1,0:T(8,128)(2,1)S(1)}, u32[]{:S(2)}, u32[]{:S(2)}) collective-permute-start(bf16[128,896]{1,0:T(8,128)(2,1)S(1)} %concatenate.76.refs_3_), channel_id=1, source_target_pairs={{0,3},{1,4},{2,5},{3,6},{4,7},{8,11},{9,12},{10,13},{11,14},{12,15... | collective-permute-start | bytes 688136 | tf_op jit(solution)/shard_map/ppermute | solution.py:75
  188.0 27.1 %collective-permute-start.21 = (bf16[128,896]{1,0:T(8,128)(2,1)S(1)}, bf16[128,896]{1,0:T(8,128)(2,1)S(1)}, u32[]{:S(2)}, u32[]{:S(2)}) collective-permute-start(bf16[128,896]{1,0:T(8,128)(2,1)S(1)} %concatenate.76.refs_3_), channel_id=1, source_target_pairs={{0,2},{1,3},{2,4},{3,5},{4,6},{5,7},{8,10},{9,11},{10,12},{11,13},... | collective-permute-start | bytes 688136 | tf_op jit(solution)/shard_map/ppermute | solution.py:75
  190.3 26.3 %collective-permute-start.22 = (bf16[128,896]{1,0:T(8,128)(2,1)S(1)}, bf16[128,896]{1,0:T(8,128)(2,1)S(1)}, u32[]{:S(2)}, u32[]{:S(2)}) collective-permute-start(bf16[128,896]{1,0:T(8,128)(2,1)S(1)} %concatenate.76.refs_3_), channel_id=1, source_target_pairs={{0,1},{1,2},{2,3},{3,4},{4,5},{5,6},{6,7},{8,9},{9,10},{10,11},{11... | collective-permute-start | bytes 688136 | tf_op jit(solution)/shard_map/ppermute | solution.py:75
  192.0 24.7 %collective-permute-start.23 = (bf16[128,896]{1,0:T(8,128)(2,1)S(1)}, bf16[128,896]{1,0:T(8,128)(2,1)}, u32[]{:S(2)}, u32[]{:S(2)}) collective-permute-start(bf16[128,896]{1,0:T(8,128)(2,1)S(1)} %concatenate.76.refs_3_), channel_id=1, source_target_pairs={{1,0},{2,1},{3,2},{4,3},{5,4},{6,5},{7,6},{9,8},{10,9},{11,10},{12... | collective-permute-start | bytes 688136 | tf_op jit(solution)/shard_map/ppermute | solution.py:75
  193.3 24.2 %collective-permute-start.24 = (bf16[128,896]{1,0:T(8,128)(2,1)S(1)}, bf16[128,896]{1,0:T(8,128)(2,1)}, u32[]{:S(2)}, u32[]{:S(2)}) collective-permute-start(bf16[128,896]{1,0:T(8,128)(2,1)S(1)} %concatenate.76.refs_3_), channel_id=1, source_target_pairs={{2,0},{3,1},{4,2},{5,3},{6,4},{7,5},{10,8},{11,9},{12,10},{13,11},... | collective-permute-start | bytes 688136 | tf_op jit(solution)/shard_map/ppermute | solution.py:75
  215.1 40.4 %collective-permute-start.33 = (bf16[384,4352]{1,0:T(8,128)(2,1)}, bf16[384,4352]{1,0:T(8,128)(2,1)}, u32[]{:S(2)}, u32[]{:S(2)}) collective-permute-start(bf16[384,4352]{1,0:T(8,128)(2,1)} %pad_maximum_fusion), channel_id=1, source_target_pairs={{0,1},{1,0},{2,3},{3,2},{4,5},{5,4},{6,7},{7,6},{8,9},{9,8},{10,11... | collective-permute-start | bytes 10027016 | tf_op jit(solution)/shard_map/ppermute | solution.py:47
  252.0 14.6 %collective-permute-start.29 = (bf16[96,2432]{1,0:T(8,128)(2,1)S(1)}, bf16[96,2432]{1,0:T(8,128)(2,1)S(1)}, u32[]{:S(2)}, u32[]{:S(2)}) collective-permute-start(bf16[96,2432]{1,0:T(8,128)(2,1)S(1)} %get-tuple-element.40), channel_id=1, source_target_pairs={{0,24},{1,25},{2,26},{3,27},{4,28},{5,29},{6,30},{7,31},{8,16},{9,... | collective-permute-start | bytes 1400840 | tf_op jit(solution)/shard_map/ppermute | solution.py:47
  254.5 22.1 %collective-permute-start.28 = (bf16[96,2432]{1,0:T(8,128)(2,1)S(1)}, bf16[96,2432]{1,0:T(8,128)(2,1)S(1)}, u32[]{:S(2)}, u32[]{:S(2)}) collective-permute-start(bf16[96,2432]{1,0:T(8,128)(2,1)S(1)} %get-tuple-element.41), channel_id=1, source_target_pairs={{0,16},{1,17},{2,18},{3,19},{4,20},{5,21},{6,22},{7,23},{8,24},{9,... | collective-permute-start | bytes 1400840 | tf_op jit(solution)/shard_map/ppermute | solution.py:47
  255.0 21.6 %collective-permute-start.27 = (bf16[96,2432]{1,0:T(8,128)(2,1)S(1)}, bf16[96,2432]{1,0:T(8,128)(2,1)S(1)}, u32[]{:S(2)}, u32[]{:S(2)}) collective-permute-start(bf16[96,2432]{1,0:T(8,128)(2,1)S(1)} %get-tuple-element.39), channel_id=1, source_target_pairs={{0,8},{1,9},{2,10},{3,11},{4,12},{5,13},{6,14},{7,15},{8,0},{9,1},... | collective-permute-start | bytes 1400840 | tf_op jit(solution)/shard_map/ppermute | solution.py:47
  258.0 36.5 %collective-permute-start.36 = (bf16[96,4352]{1,0:T(8,128)(2,1)S(1)}, bf16[96,4352]{1,0:T(8,128)(2,1)S(1)}, u32[]{:S(2)}, u32[]{:S(2)}) collective-permute-start(bf16[96,4352]{1,0:T(8,128)(2,1)S(1)} %get-tuple-element.37), channel_id=1, source_target_pairs={{0,24},{1,25},{2,26},{3,27},{4,28},{5,29},{6,30},{7,31},{8,16},{9,... | collective-permute-start | bytes 2506760 | tf_op jit(solution)/shard_map/ppermute | solution.py:47
  260.5 51.6 %collective-permute-start.35 = (bf16[96,4352]{1,0:T(8,128)(2,1)S(1)}, bf16[96,4352]{1,0:T(8,128)(2,1)S(1)}, u32[]{:S(2)}, u32[]{:S(2)}) collective-permute-start(bf16[96,4352]{1,0:T(8,128)(2,1)S(1)} %get-tuple-element.38), channel_id=1, source_target_pairs={{0,16},{1,17},{2,18},{3,19},{4,20},{5,21},{6,22},{7,23},{8,24},{9,... | collective-permute-start | bytes 2506760 | tf_op jit(solution)/shard_map/ppermute | solution.py:47
  266.5 45.7 %collective-permute-start.34 = (bf16[96,4352]{1,0:T(8,128)(2,1)S(1)}, bf16[96,4352]{1,0:T(8,128)(2,1)S(1)}, u32[]{:S(2)}, u32[]{:S(2)}) collective-permute-start(bf16[96,4352]{1,0:T(8,128)(2,1)S(1)} %get-tuple-element.36), channel_id=1, source_target_pairs={{0,8},{1,9},{2,10},{3,11},{4,12},{5,13},{6,14},{7,15},{8,0},{9,1},... | collective-permute-start | bytes 2506760 | tf_op jit(solution)/shard_map/ppermute | solution.py:47
  276.9 37.3 %collective-permute-start.32 = (bf16[24,2432]{1,0:T(8,128)(2,1)S(1)}, bf16[24,2432]{1,0:T(8,128)(2,1)S(1)}, u32[]{:S(2)}, u32[]{:S(2)}) collective-permute-start(bf16[24,2432]{1,0:T(8,128)(2,1)S(1)} %get-tuple-element.52), channel_id=1, source_target_pairs={{0,6},{1,7},{2,4},{3,5},{4,2},{5,3},{6,0},{7,1},{8,14},{9,15},{10,... | collective-permute-start | bytes 350216 | tf_op jit(solution)/shard_map/ppermute | solution.py:47
  277.0 40.2 %collective-permute-start.31 = (bf16[24,2432]{1,0:T(8,128)(2,1)S(1)}, bf16[24,2432]{1,0:T(8,128)(2,1)S(1)}, u32[]{:S(2)}, u32[]{:S(2)}) collective-permute-start(bf16[24,2432]{1,0:T(8,128)(2,1)S(1)} %get-tuple-element.53), channel_id=1, source_target_pairs={{0,4},{1,5},{2,6},{3,7},{4,0},{5,1},{6,2},{7,3},{8,12},{9,13},{10,... | collective-permute-start | bytes 350216 | tf_op jit(solution)/shard_map/ppermute | solution.py:47
  294.5 22.6 %collective-permute-start.30 = (bf16[24,2432]{1,0:T(8,128)(2,1)S(1)}, bf16[24,2432]{1,0:T(8,128)(2,1)S(1)}, u32[]{:S(2)}, u32[]{:S(2)}) collective-permute-start(bf16[24,2432]{1,0:T(8,128)(2,1)S(1)} %get-tuple-element.51), channel_id=1, source_target_pairs={{0,2},{1,3},{2,0},{3,1},{4,6},{5,7},{6,4},{7,5},{8,10},{9,11},{10,... | collective-permute-start | bytes 350216 | tf_op jit(solution)/shard_map/ppermute | solution.py:47
  312.8 19.7 %collective-permute-start.38 = (bf16[24,4352]{1,0:T(8,128)(2,1)S(1)}, bf16[24,4352]{1,0:T(8,128)(2,1)S(1)}, u32[]{:S(2)}, u32[]{:S(2)}) collective-permute-start(bf16[24,4352]{1,0:T(8,128)(2,1)S(1)} %get-tuple-element.49), channel_id=1, source_target_pairs={{0,4},{1,5},{2,6},{3,7},{4,0},{5,1},{6,2},{7,3},{8,12},{9,13},{10,... | collective-permute-start | bytes 626696 | tf_op jit(solution)/shard_map/ppermute | solution.py:47
  314.1 18.4 %collective-permute-start.37 = (bf16[24,4352]{1,0:T(8,128)(2,1)S(1)}, bf16[24,4352]{1,0:T(8,128)(2,1)S(1)}, u32[]{:S(2)}, u32[]{:S(2)}) collective-permute-start(bf16[24,4352]{1,0:T(8,128)(2,1)S(1)} %get-tuple-element.47), channel_id=1, source_target_pairs={{0,2},{1,3},{2,0},{3,1},{4,6},{5,7},{6,4},{7,5},{8,10},{9,11},{10,... | collective-permute-start | bytes 626696 | tf_op jit(solution)/shard_map/ppermute | solution.py:47
  (52 other events, 584.3 us)
